TPU v7x, 512 devices: a whole 4x8x8 slice. The times are simulated.
512 devices in a mesh: dp: 64 (over z, y_hi, core), ctx: 8 (over y_lo, x).
Axes of the slice: x: 4, y: 8 (y_hi: 4, y_lo: 2; y = y_hi * 2 + y_lo), z: 8, core: 2. Of those that a mesh axis runs over, the one named last changes fastest.
Arguments:
- glu_in: bfloat16 [64, 1024, 1536], P('dp', 'ctx'), may hold values from -40 to 40
- lengths: int32 [64], P('dp'), may hold values from 512 to 1024, as said below
- kernel: float32 [31, 768], replicated, may hold values from -1 to 1
- bn_gain: float32 [768], replicated, may hold values from 0.1 to 1.9
- bn_bias: float32 [768], replicated, may hold values from -1 to 1
- proj_weight: bfloat16 [768, 768], P('dp'), may hold values from -0.21875 to 0.21875
- cotangent: bfloat16 [64, 1024, 768], P('dp', 'ctx'), may hold values from -6 to 6
Outputs:
- out: bfloat16 [64, 1024, 768], P('dp', 'ctx')
- grad_glu_in: bfloat16 [64, 1024, 1536], P('dp', 'ctx')
- grad_proj: float32 [768, 768], P('dp')
- grad_kernel: float32 [31, 768], replicated
- grad_gain: float32 [768], replicated
- grad_bias: float32 [768], replicated
Inputs may be any that keep to these rules, and one draw needn't show every extreme that they name: `lengths`: positions below a sequence's length are real tokens and the rest padding; some sequence is full and some has exactly 512 valid positions.
All inputs are finite; a program needn't handle non-finite values.
Results may differ from a plain program's by a relative error of at most 0.013.
Values may be sent and summed in bfloat16 or wider, within the bound.
A program may use at most 64 MiB of HBM per device.

v0:
```python
import jax
import jax.numpy as jnp
from jax import lax
from jax.sharding import PartitionSpec as P

eps = 1e-05


def extended(cells, sides, width):
    for axis, dim in sides:
        count = lax.axis_size(axis)
        ends = count - 1
        head = lax.slice_in_dim(cells, 0, width, axis=dim)
        tail = lax.slice_in_dim(cells, cells.shape[dim] - width, cells.shape[dim], axis=dim)
        cells = jnp.concatenate(
            [
                lax.ppermute(tail, axis, [(i, (i + 1) % count) for i in range(ends)]),
                cells,
                lax.ppermute(head, axis, [((i + 1) % count, i) for i in range(ends)]),
            ],
            axis=dim,
        )
    return cells


def body(glu_in, lengths, kernel, bn_gain, bn_bias, proj_weight, cotangent):
    tokens = glu_in.shape[1]
    channels = glu_in.shape[2] // 2
    taps = kernel.shape[0]
    reach = (taps - 1) // 2
    rows = glu_in[0]
    value = rows[:, :channels].astype(jnp.float32)
    gate = rows[:, channels:].astype(jnp.float32)
    positions = lax.axis_index("ctx") * tokens + jnp.arange(tokens, dtype=jnp.int32)
    live = (positions < lengths[0]).astype(jnp.float32)[:, None]
    sig_gate = jax.nn.sigmoid(gate)
    unit_out = (live * value * sig_gate).astype(jnp.bfloat16)
    padded_unit = extended(unit_out, (("ctx", 0),), reach).astype(jnp.float32)
    conv = jnp.zeros((tokens, channels), jnp.float32)
    for shift_k in range(taps):
        conv = conv + kernel[shift_k] * padded_unit[shift_k : shift_k + tokens]
    total_z, count = lax.psum((jnp.sum(live * conv, 0), jnp.sum(live)), ("dp", "ctx"))
    mean = total_z / count
    centered = conv - mean
    var_sum = lax.psum(jnp.sum(live * centered * centered, 0), ("dp", "ctx"))
    variance = var_sum / count
    inv_std = lax.rsqrt(variance + eps)
    normed = centered * inv_std
    pre = bn_gain * normed + bn_bias
    sig_pre = jax.nn.sigmoid(pre)
    act = (live * pre * sig_pre).astype(jnp.bfloat16)
    upstream = cotangent[0]
    projected = jnp.dot(
        act,
        lax.all_gather(proj_weight, "dp", axis=0, tiled=True),
        preferred_element_type=jnp.float32,
    )
    d_act = jnp.einsum(
        "td,cd->tc",
        upstream,
        lax.all_gather(proj_weight, "dp", axis=0, tiled=True),
        preferred_element_type=jnp.float32,
    )
    result = projected.astype(jnp.bfloat16)[None]
    d_pre = live * d_act * sig_pre * (1.0 + pre * (1.0 - sig_pre))
    sum_bias, sum_gain = lax.psum((jnp.sum(d_pre, 0), jnp.sum(d_pre * normed, 0)), ("dp", "ctx"))
    d_conv = (
        live * bn_gain * inv_std * (d_pre - sum_bias / count - normed * sum_gain / count)
    ).astype(jnp.bfloat16)
    padded_grad = extended(d_conv, (("ctx", 0),), reach).astype(jnp.float32)
    d_wide = d_conv.astype(jnp.float32)
    terms = jnp.stack(
        [jnp.sum(d_wide * padded_unit[shift_k : shift_k + tokens], 0) for shift_k in range(taps)]
    )
    kernel_sum = lax.psum(terms, ("dp", "ctx"))
    d_unit = jnp.zeros((tokens, channels), jnp.float32)
    for shift_k in range(taps):
        first = taps - 1 - shift_k
        d_unit = d_unit + kernel[shift_k] * padded_grad[first : first + tokens]
    d_unit = live * d_unit
    grad_glu = jnp.concatenate(
        [d_unit * sig_gate, d_unit * value * sig_gate * (1.0 - sig_gate)], 1
    ).astype(jnp.bfloat16)[None]
    term = jnp.einsum("tc,td->cd", act, upstream, preferred_element_type=jnp.float32)
    merged = lax.psum(term.astype(jnp.bfloat16), "ctx").astype(jnp.float32)
    owned = lax.psum_scatter(merged, "dp", scatter_dimension=0, tiled=True)
    scale = lax.rsqrt(count)
    return (result, grad_glu, owned * scale, kernel_sum * scale, sum_gain * scale, sum_bias * scale)


def solution(mesh):
    in_specs = (P("dp", "ctx", None), P("dp"), P(), P(), P(), P("dp", None), P("dp", "ctx", None))
    out_specs = (P("dp", "ctx", None), P("dp", "ctx", None), P("dp", None), P(), P(), P())
    return jax.shard_map(body, mesh=mesh, in_specs=in_specs, out_specs=out_specs, check_vma=False)
```

profile of v0, /device:TPU:1, one launch (start us, length us, event | category | flops | bytes accessed | tf_op | source)
XLA Modules:
  0.0 907.7 jit_solution(10261338319502410541)
XLA Ops:
  8.8 0.6 fusion.78
  9.4 1.2 fusion.5
  10.5 3.9 collective-permute-start
  14.5 1.3 collective-permute-start.1
  15.8 1.4 slice_reduce_fusion.30
  17.2 1.1 slice_reduce_fusion.29
  19.1 1.1 multiply_reduce_fusion.1
  20.4 106.7 %all-reduce.3 = (f32[768]{0:T(1024)S(1)}, f32[]{:T(128)}) all-reduce(f32[768]{0:T(1024)S(1)} %get-tuple-element.79, f32[]{:T(128)} %get-tuple-element.77), channel_id=1, replica_groups=mesh['dp'=64,'ctx'=8] {'dp','ctx'}, use_global_device_ids=true, to_apply=%region_1.0 | all-reduce | flops 769 | bytes 6152 | tf_op jit(solution)/shard_map/psum | solution.py:42
  127.1 0.6 broadcast_divide_fusion.1
  127.9 94.6 %psum.51 = f32[768]{0:T(1024)S(1)} all-reduce(f32[768]{0:T(1024)S(1)} %fusion.9), channel_id=1, replica_groups=mesh['dp'=64,'ctx'=8] {'dp','ctx'}, use_global_device_ids=true, to_apply=%region_5.0 | all-reduce | flops 768 | bytes 6144 | tf_op jit(solution)/shard_map/psum | solution.py:45
  222.6 0.7 add_rsqrt_fusion
  223.3 1.6 convolution_convert_fusion
  225.5 80.6 %all-reduce.7.cloned.1.call-done = bf16[768,768]{1,0:T(8,128)(2,1)} async-done(((bf16[768,768]{1,0:T(8,128)(2,1)}), bf16[768,768]{1,0:T(8,128)(2,1)}) %all-reduce.7.cloned.1.call-update) | async-done | bytes 1179664 | tf_op jit(solution)/shard_map/psum | solution.py:85
  306.1 1.4 convert_element_type.59
  307.6 160.0 %fusion = f32[16,768]{1,0:T(8,128)S(1)} fusion(f32[768,768]{1,0:T(8,128)S(1)} %convert_element_type.59), kind=kCustom, calls=%all-reduce-scatter | all-reduce-scatter fusion | flops 786433 | bytes 2410496
  467.6 1.3 collective-permute-start.19
  468.9 14.3 %collective-permute-start.18 = (f32[16,768]{1,0:T(8,128)S(1)}, f32[16,768]{1,0:T(8,128)S(1)}, u32[]{:S(2)}, u32[]{:S(2)}) collective-permute-start(f32[16,768]{1,0:T(8,128)S(1)} %fusion), channel_id=1, source_target_pairs={{0,120},{8,128},{16,136},{24,144},{32,152},{40,160},{48,168},{56,1... | collective-permute-start | bytes 147464
  483.2 1.3 collective-permute-start.17
  484.5 1.3 collective-permute-start.16
  485.8 1.3 collective-permute-start.15
  487.1 1.3 collective-permute-start.14
  488.4 8.7 collective-permute-start.13
  497.1 3.1 collective-permute-start.12
  500.2 1.3 collective-permute-start.11
  501.5 1.3 collective-permute-start.10
  502.8 2.9 collective-permute-start.9
  505.7 3.6 collective-permute-start.8
  509.3 4.5 collective-permute-start.7
  513.8 4.5 collective-permute-start.6
  518.3 2.8 collective-permute-start.5
  521.2 1.9 collective-permute-start.4
  523.1 1.3 dynamic-slice.4
  525.8 2.1 concatenate.26
  527.8 0.6 dynamic-slice_multiply_fusion
  528.5 2.3 reshape.56
  530.8 1.1 fusion.3
  532.5 97.9 %all-reduce.2 = (f32[768]{0:T(1024)S(1)}, f32[768]{0:T(1024)S(1)}) all-reduce(f32[768]{0:T(1024)S(1)} %get-tuple-element.38, f32[768]{0:T(1024)S(1)} %get-tuple-element.37), channel_id=1, replica_groups=mesh['dp'=64,'ctx'=8] {'dp','ctx'}, use_global_device_ids=true, to_apply=%region_9.0 | all-reduce | flops 1536 | bytes 12288 | tf_op jit(solution)/shard_map/psum | solution.py:66
  630.4 1.2 broadcast_multiply_fusion.1
  631.7 1.6 fusion.40
  633.3 0.6 fusion.39
  634.1 1.7 collective-permute-start.2
  635.7 1.3 collective-permute-start.3
  637.0 0.6 broadcast_multiply_fusion.2
  638.0 2.6 stack.127
  640.8 1.3 fusion.72
  642.3 0.8 pad_maximum_fusion
  643.1 255.6 %all-reduce.9.cloned.1.call-done = f32[31,768]{1,0:T(8,128)} async-done(((f32[31,768]{1,0:T(8,128)}), f32[31,768]{1,0:T(8,128)}) %all-reduce.9.cloned.1.call-update) | async-done | bytes 95248 | tf_op jit(solution)/shard_map/psum | solution.py:75
  898.7 1.5 broadcast_multiply_fusion
  (150 shorter events, 2.6 us)
Async XLA Ops:
  8.0 215.2 %copy-start = (bf16[1,128,768]{2,1,0:T(8,128)(2,1)S(1)}, bf16[1,128,768]{2,1,0:T(8,128)(2,1)}, u32[]{:S(2)}) copy-start(bf16[1,128,768]{2,1,0:T(8,128)(2,1)} %param.13) | copy-start | bytes 589828
  8.0 298.1 %all-reduce.7.cloned.1.call-start = ((), (), s32[]{:S(2)}) async-start(), calls=%async_computation | async-start | bytes 2359296 | tf_op jit(solution)/shard_map/psum | solution.py:85
  9.4 213.9 %copy-start.34 = (f32[128]{0:T(128)}, f32[128]{0:T(128)S(1)}, u32[]{:S(2)}) copy-start(f32[128]{0:T(128)S(1)} %get-tuple-element.78) | copy-start | bytes 1540
  10.5 8.0 collective-permute-start
  14.5 4.6 collective-permute-start.1
  17.2 3.1 copy-start.2
  17.2 3.1 copy-start.4
  17.2 3.1 copy-start.6
  19.1 204.1 %copy-start.38 = (f32[768]{0:T(1024)S(1)}, f32[768]{0:T(1024)}, u32[]{:S(2)}) copy-start(f32[768]{0:T(1024)} %param.10) | copy-start | bytes 9220
  19.1 204.1 %copy-start.40 = (f32[768]{0:T(1024)S(1)}, f32[768]{0:T(1024)}, u32[]{:S(2)}) copy-start(f32[768]{0:T(1024)} %param.11) | copy-start | bytes 9220
  127.8 97.1 %copy-start.32 = (f32[768]{0:T(1024)}, f32[768]{0:T(1024)S(1)}, u32[]{:S(2)}) copy-start(f32[768]{0:T(1024)S(1)} %broadcast_divide_fusion.1) | copy-start | bytes 9220
  224.9 303.6 %all-gather.3.cloned.1.call-start = ((), (), s32[]{:S(2)}) async-start(), calls=%async_computation.2 | async-start | bytes 1597440 | tf_op jit(solution)/shard_map/all_gather | solution.py:55
  225.5 673.2 %all-reduce.9.cloned.1.call-start = ((), (), s32[]{:S(2)}) async-start(), calls=%async_computation.1 | async-start | bytes 196608 | tf_op jit(solution)/shard_map/psum | solution.py:75
  467.6 19.5 %collective-permute-start.19 = (f32[12,768]{1,0:T(8,128)S(1)}, f32[12,768]{1,0:T(8,128)S(1)}, u32[]{:S(2)}, u32[]{:S(2)}) collective-permute-start(f32[12,768]{1,0:T(8,128)S(1)} %slice.526), channel_id=1, source_target_pairs={{0,128},{8,136},{16,144},{24,152},{32,160},{40,168},{48,176},{56,1... | collective-permute-start | bytes 110600
  468.9 19.5 %collective-permute-start.18 = (f32[16,768]{1,0:T(8,128)S(1)}, f32[16,768]{1,0:T(8,128)S(1)}, u32[]{:S(2)}, u32[]{:S(2)}) collective-permute-start(f32[16,768]{1,0:T(8,128)S(1)} %fusion), channel_id=1, source_target_pairs={{0,120},{8,128},{16,136},{24,144},{32,152},{40,160},{48,168},{56,1... | collective-permute-start | bytes 147464
  483.2 13.9 %collective-permute-start.17 = (f32[16,768]{1,0:T(8,128)S(1)}, f32[16,768]{1,0:T(8,128)S(1)}, u32[]{:S(2)}, u32[]{:S(2)}) collective-permute-start(f32[16,768]{1,0:T(8,128)S(1)} %fusion), channel_id=1, source_target_pairs={{0,112},{8,120},{16,128},{24,136},{32,144},{40,152},{48,160},{56,1... | collective-permute-start | bytes 147464
  484.5 15.7 %collective-permute-start.16 = (f32[16,768]{1,0:T(8,128)S(1)}, f32[16,768]{1,0:T(8,128)S(1)}, u32[]{:S(2)}, u32[]{:S(2)}) collective-permute-start(f32[16,768]{1,0:T(8,128)S(1)} %fusion), channel_id=1, source_target_pairs={{0,104},{8,112},{16,120},{24,128},{32,136},{40,144},{48,152},{56,1... | collective-permute-start | bytes 147464
  485.8 15.7 %collective-permute-start.15 = (f32[16,768]{1,0:T(8,128)S(1)}, f32[16,768]{1,0:T(8,128)S(1)}, u32[]{:S(2)}, u32[]{:S(2)}) collective-permute-start(f32[16,768]{1,0:T(8,128)S(1)} %fusion), channel_id=1, source_target_pairs={{0,96},{8,104},{16,112},{24,120},{32,128},{40,136},{48,144},{56,15... | collective-permute-start | bytes 147464
  487.1 15.7 %collective-permute-start.14 = (f32[16,768]{1,0:T(8,128)S(1)}, f32[16,768]{1,0:T(8,128)S(1)}, u32[]{:S(2)}, u32[]{:S(2)}) collective-permute-start(f32[16,768]{1,0:T(8,128)S(1)} %fusion), channel_id=1, source_target_pairs={{0,88},{8,96},{16,104},{24,112},{32,120},{40,128},{48,136},{56,144... | collective-permute-start | bytes 147464
  488.4 17.3 %collective-permute-start.13 = (f32[16,768]{1,0:T(8,128)S(1)}, f32[16,768]{1,0:T(8,128)S(1)}, u32[]{:S(2)}, u32[]{:S(2)}) collective-permute-start(f32[16,768]{1,0:T(8,128)S(1)} %fusion), channel_id=1, source_target_pairs={{0,80},{8,88},{16,96},{24,104},{32,112},{40,120},{48,128},{56,136}... | collective-permute-start | bytes 147464
  497.1 12.2 %collective-permute-start.12 = (f32[16,768]{1,0:T(8,128)S(1)}, f32[16,768]{1,0:T(8,128)S(1)}, u32[]{:S(2)}, u32[]{:S(2)}) collective-permute-start(f32[16,768]{1,0:T(8,128)S(1)} %fusion), channel_id=1, source_target_pairs={{0,72},{8,80},{16,88},{24,96},{32,104},{40,112},{48,120},{56,128},... | collective-permute-start | bytes 147464
  500.2 13.7 %collective-permute-start.11 = (f32[16,768]{1,0:T(8,128)S(1)}, f32[16,768]{1,0:T(8,128)S(1)}, u32[]{:S(2)}, u32[]{:S(2)}) collective-permute-start(f32[16,768]{1,0:T(8,128)S(1)} %fusion), channel_id=1, source_target_pairs={{0,64},{8,72},{16,80},{24,88},{32,96},{40,104},{48,112},{56,120},{... | collective-permute-start | bytes 147464
  501.5 16.8 %collective-permute-start.10 = (f32[16,768]{1,0:T(8,128)S(1)}, f32[16,768]{1,0:T(8,128)S(1)}, u32[]{:S(2)}, u32[]{:S(2)}) collective-permute-start(f32[16,768]{1,0:T(8,128)S(1)} %fusion), channel_id=1, source_target_pairs={{0,56},{8,64},{16,72},{24,80},{32,88},{40,96},{48,104},{56,112},{6... | collective-permute-start | bytes 147464
  502.8 18.4 %collective-permute-start.9 = (f32[16,768]{1,0:T(8,128)S(1)}, f32[16,768]{1,0:T(8,128)S(1)}, u32[]{:S(2)}, u32[]{:S(2)}) collective-permute-start(f32[16,768]{1,0:T(8,128)S(1)} %fusion), channel_id=1, source_target_pairs={{0,48},{8,56},{16,64},{24,72},{32,80},{40,88},{48,96},{56,104},{64... | collective-permute-start | bytes 147464
  505.7 20.0 %collective-permute-start.8 = (f32[16,768]{1,0:T(8,128)S(1)}, f32[16,768]{1,0:T(8,128)S(1)}, u32[]{:S(2)}, u32[]{:S(2)}) collective-permute-start(f32[16,768]{1,0:T(8,128)S(1)} %fusion), channel_id=1, source_target_pairs={{0,40},{8,48},{16,56},{24,64},{32,72},{40,80},{48,88},{56,96},{64,... | collective-permute-start | bytes 147464
  509.3 16.4 %collective-permute-start.7 = (f32[16,768]{1,0:T(8,128)S(1)}, f32[16,768]{1,0:T(8,128)S(1)}, u32[]{:S(2)}, u32[]{:S(2)}) collective-permute-start(f32[16,768]{1,0:T(8,128)S(1)} %fusion), channel_id=1, source_target_pairs={{0,32},{8,40},{16,48},{24,56},{32,64},{40,72},{48,80},{56,88},{64,... | collective-permute-start | bytes 147464
  513.8 11.9 %collective-permute-start.6 = (f32[16,768]{1,0:T(8,128)S(1)}, f32[16,768]{1,0:T(8,128)S(1)}, u32[]{:S(2)}, u32[]{:S(2)}) collective-permute-start(f32[16,768]{1,0:T(8,128)S(1)} %fusion), channel_id=1, source_target_pairs={{0,24},{8,32},{16,40},{24,48},{32,56},{40,64},{48,72},{56,80},{64,... | collective-permute-start | bytes 147464
  518.3 7.4 collective-permute-start.5
  521.2 4.6 collective-permute-start.4
  528.5 2.4 copy-start.41
  633.9 6.8 copy-start.1
  633.9 6.8 copy-start.3
  633.9 6.8 copy-start.5
  633.9 6.8 copy-start.7
  633.9 6.8 copy-start.9
  633.9 6.8 copy-start.11
  634.0 6.8 copy-start.13
  634.0 6.8 copy-start.15
  634.0 6.8 copy-start.17
  634.0 6.8 copy-start.19
  634.0 6.8 copy-start.21
  634.0 6.8 copy-start.23
  634.0 6.8 copy-start.25
  634.0 6.8 copy-start.27
  634.0 6.8 copy-start.29
  634.0 6.8 copy-start.31
  634.1 6.5 collective-permute-start.2
  635.7 4.9 collective-permute-start.3
  (17 other events, 34.2 us)
Sparse Core Ops, SparseCore 0:
  225.0 81.0 all-reduce.6
Sparse Core Ops, SparseCore 1:
  228.7 79.3 all-gather.2
  640.7 257.9 all-reduce.8
where the time goes:
time: 909 us; the launch traced here: 908 us
  blocking collectives  459 us (50%)
  waiting for transfers between devices  337 us (37%)
  starting transfers between devices  63.6 us (7%)
  between operations  18.8 us (2%)
  other arithmetic  14.3 us (2%)
  local copies, waits for them, and re-layouts  11.1 us (1%)
    psum x1, waiting for transfers between devices, body(): kernel_sum = lax.psum(terms, ('dp', 'ctx'))  256 us
    unnamed x1, blocking collectives  160 us
    psum x1, blocking collectives, body(): lax.psum((jnp.sum(live * conv, 0), jnp.sum(live)), ('dp', 'ctx'))  107 us
    psum x1, blocking collectives, body(): lax.psum((jnp.sum(d_pre, 0), jnp.sum(d_pre * normed, 0)), ('dp', 'ctx'))  97.9 us
    psum x1, blocking collectives, body(): var_sum = lax.psum(jnp.sum(live * centered * centered, 0), ('dp', 'ctx'))  94.6 us
    psum x1, waiting for transfers between devices, body(): merged = lax.psum(term.astype(jnp.bfloat16), 'ctx').astype(jnp.float32)  80.6 us
    unnamed x16, starting transfers between devices  55.3 us
  transfers between devices with their start and end apart: 23, of which 3 were waited for; matrix products, arithmetic and copies ran while one was open for 19% of the time, Pallas kernels for 0%

commit v1 on v0

v1 whole, which is shorter than its diff:
```python
import functools

import jax
import jax.numpy as jnp
from jax import lax
from jax.experimental import pallas as pl
from jax.experimental.pallas import tpu as pltpu
from jax.sharding import PartitionSpec as P

eps = 1e-05
f32 = jnp.float32
bf16 = jnp.bfloat16

NZ, NYH, NC, NYL, NX = 8, 4, 2, 2, 4
ROWS, CH, TAPS, LANES = 128, 768, 31, 128
TILES = CH // LANES
HALF = CH // 2
REACH = 16
BLOCK = CH // (NZ * NYH * NC)


def rem(a, b):
    return lax.rem(a, jnp.int32(b))


def div(a, b):
    return lax.div(a, jnp.int32(b))


def lanes_of(c, first=0):
    return pl.ds(pl.multiple_of(first + c * LANES, LANES), LANES)


def tiles(fn):
    def step(c, carry):
        fn(c)
        return carry

    lax.fori_loop(0, TILES, step, 0)


def fused(glu_hbm, len_ref, kern_hbm, gain_ref, bias_ref, w_hbm, cot_hbm,
          out_hbm, gg_hbm, gp_ref, gk_ref, gn_ref, gb_ref,
          glu, cot, kern, unit, conv, fac, dwide, da, act, out, gg,
          wblk, wfull, hs, hr, ds_, dr_, a1, a2, a3, b1, b2, b3, stat,
          kt, kr, k2, k3, kf, gown, gsend, grc, gxs, gxr, gyf, gys, gyr, gz, gzr, fin, fb,
          ssem, rsem, lsem):
    dp = lax.axis_index("dp")
    ctx = lax.axis_index("ctx")
    z, yh, core = div(dp, 8), rem(div(dp, 2), 4), rem(dp, 2)
    yl, x = div(ctx, 4), rem(ctx, 4)
    y = yh * 2 + yl
    g = x * 2 + core
    sib = 1 - core

    def dev(z_, y_, x_, c_):
        return (z_ * 8 + div(y_, 2) * 2 + c_, rem(y_, 2) * 4 + x_)

    def on_g(j):
        return dev(z, y, div(j, 2), rem(j, 2))

    def on_y(j):
        return dev(z, j, x, core)

    def on_z(j):
        return dev(j, y, x, core)

    def on_x(j):
        return dev(z, y, j, core)

    sibling = dev(z, y, x, sib)
    sends = [0]
    recvs = [0]
    pending = []

    def rsems(n):
        recvs[0] += n
        return recvs[0] - n

    def copy(src, dst, recv, target):
        sends[0] += 1
        return pltpu.make_async_remote_copy(
            src_ref=src, dst_ref=dst, send_sem=ssem.at[sends[0] - 1], recv_sem=rsem.at[recv],
            device_id=target, device_id_type=pl.DeviceIdType.MESH)

    def send(src, dst, recv, target):
        c = copy(src, dst, recv, target)
        c.start()
        pending.append(c)

    def arrived(dst, recv):
        pltpu.make_async_remote_copy(
            src_ref=dst, dst_ref=dst, send_sem=ssem.at[0], recv_sem=rsem.at[recv],
            device_id=sibling, device_id_type=pl.DeviceIdType.MESH).wait_recv()

    def exchange(buf, me, where, n=8):
        base = rsems(n)
        for d in range(1, n):
            send(buf.at[me], buf.at[me], base + d, where(rem(me + d, n)))

        def done():
            for d in range(1, n):
                arrived(buf.at[rem(me + (n - d), n)], base + d)

        return done

    loads = [pltpu.make_async_copy(a, b, lsem.at[i]) for i, (a, b) in enumerate(
        [(glu_hbm, glu), (kern_hbm, kern), (cot_hbm, cot)])]
    for c in loads:
        c.start()
    load_w = pltpu.make_async_copy(w_hbm, wblk.at[z, x, core], lsem.at[3])

    @pl.when(yh == x)
    def _():
        load_w.start()

    barrier = pltpu.get_barrier_semaphore()
    peers = [on_g(rem(g + d, 8)) for d in range(1, 8)]
    peers += [on_y(rem(y + d, 8)) for d in range(1, 8)]
    peers += [on_z(rem(z + d, 8)) for d in range(1, 8)]
    flip = yh * 2 + (1 - yl)
    peers += [dev(z, flip, div(rem(g + d, 8), 2), rem(rem(g + d, 8), 2)) for d in range(1, 8)]
    for p in peers:
        pl.semaphore_signal(barrier, inc=1, device_id=p, device_id_type=pl.DeviceIdType.MESH)

    pos0 = ctx * ROWS
    length = len_ref[0]
    n_live = jnp.clip(length - pos0, 0, ROWS).astype(f32)

    def live():
        return (lax.broadcasted_iota(jnp.int32, (ROWS, LANES), 0) + pos0 < length).astype(f32)

    loads[0].wait()

    @tiles
    def _(c):
        v = glu[:, lanes_of(c)].astype(f32)
        sg = jax.nn.sigmoid(glu[:, lanes_of(c, CH)].astype(f32))
        u = (live() * v * sg).astype(bf16)
        hs[0, :, lanes_of(c)] = u[:REACH]
        hs[1, :, lanes_of(c)] = u[ROWS - REACH:]
        unit[c, pl.ds(REACH, ROWS), :] = u.astype(f32)

    @pl.when(ctx == 0)
    def _():
        hr[0] = jnp.zeros((REACH, CH), bf16)
        dr_[0] = jnp.zeros((REACH, CH), bf16)

    @pl.when(ctx == 7)
    def _():
        hr[1] = jnp.zeros((REACH, CH), bf16)
        dr_[1] = jnp.zeros((REACH, CH), bf16)

    pl.semaphore_wait(barrier, len(peers))

    def halo(src, dst):
        base = rsems(2)
        to_left = copy(src.at[0], dst.at[1], base + 1, (dp, ctx - 1))
        to_right = copy(src.at[1], dst.at[0], base, (dp, ctx + 1))

        @pl.when(ctx > 0)
        def _():
            to_left.start()

        @pl.when(ctx < 7)
        def _():
            to_right.start()

        def done():
            @pl.when(ctx > 0)
            def _():
                arrived(dst.at[0], base)
                to_left.wait_send()

            @pl.when(ctx < 7)
            def _():
                arrived(dst.at[1], base + 1)
                to_right.wait_send()

        return done

    halo_done = halo(hs, hr)

    w1 = rsems(1)
    mine = wblk.at[z, x, core]
    w1_sends = [copy(mine, mine, w1, on_y(rem(yh + d, 4) * 2 + yl)) for d in range(1, 4)]

    @pl.when(yh == x)
    def _():
        load_w.wait()
        for c in w1_sends:
            c.start()

    @pl.when(yh != x)
    def _():
        arrived(mine, w1)

    w2 = rsems(8)
    for d in range(1, 8):
        send(mine, mine, w2 + d, on_z(rem(z + d, 8)))

    halo_done()
    loads[1].wait()

    @tiles
    def _(c):
        unit[c, pl.ds(0, REACH), :] = hr[0, :, lanes_of(c)].astype(f32)
        unit[c, pl.ds(REACH + ROWS, REACH), :] = hr[1, :, lanes_of(c)].astype(f32)
        acc = jnp.zeros((ROWS, LANES), f32)
        for k in range(TAPS):
            acc = acc + kern[pl.ds(k, 1), lanes_of(c)] * unit[c, pl.ds(k + 1, ROWS), :]
        conv[c] = acc
        m = live()
        s = jnp.sum(m * acc, 0, keepdims=True)
        centred = acc - s / jnp.maximum(n_live, 1.0)
        q = jnp.sum(m * centred * centred, 0, keepdims=True)
        n = jnp.full((1, LANES), n_live, f32)
        a1[g, :, lanes_of(c)] = jnp.concatenate([s, q, n, jnp.zeros((1, LANES), f32)], 0)

    def merged(buf):
        total = buf[0]
        for i in range(1, 8):
            total = total + buf[i]
        s, q, n = total[0:1], total[1:2], total[2:3]
        mean = s / jnp.maximum(n, 1.0)
        for i in range(8):
            off = buf[i, 0:1, :] - buf[i, 2:3, :] * mean
            q = q + off * off / jnp.maximum(buf[i, 2:3, :], 1.0)
        return s, q, n

    def summed(buf):
        total = buf[0]
        for i in range(1, 8):
            total = total + buf[i]
        return total

    a_done = exchange(a1, g, on_g)
    for d in range(1, 8):
        arrived(wblk.at[rem(z + (8 - d), 8), x, core], w2 + d)
    w3 = rsems(4)
    w4 = rsems(4)
    strip = wblk.at[:, x, core]
    for d in range(1, 4):
        send(strip, strip, w3 + d, on_x(rem(x + d, 4)))
    send(strip, strip, w4, sibling)

    zero = jnp.zeros((1, CH), f32)
    a_done()
    a2[y] = jnp.concatenate([*merged(a1), zero], 0)
    a_done = exchange(a2, y, on_y)
    a_done()
    a3[z] = jnp.concatenate([*merged(a2), zero], 0)
    a_done = exchange(a3, z, on_z)
    for d in range(1, 4):
        piece = wblk.at[:, rem(x + (4 - d), 4), core]
        arrived(piece, w3 + d)
        send(piece, piece, w4 + d, sibling)
    a_done()
    s, q, n = merged(a3)
    stat[0:1] = s / n
    stat[1:2] = lax.rsqrt(q / n + eps)
    stat[2:3] = 1.0 / n
    stat[3:4] = lax.rsqrt(n)

    @tiles
    def _(c):
        at = lanes_of(c)
        normed = (conv[c] - stat[0:1, at]) * stat[1:2, at]
        conv[c] = normed
        pre = gain_ref[0:1, at] * normed + bias_ref[0:1, at]
        sp = jax.nn.sigmoid(pre)
        m = live()
        act[:, at] = (m * pre * sp).astype(bf16)
        fac[c] = m * sp * (1.0 + pre * (1.0 - sp))

    for d in range(4):
        arrived(wblk.at[:, rem(x + (4 - d), 4), sib], w4 + d)

    def gather(i, carry):
        for p in range(2):
            rows = jnp.concatenate(
                [wblk[i, 2 * p + h, e].astype(f32) for h in range(2) for e in range(2)], 0)
            wfull[pl.ds(pl.multiple_of(i * 96 + p * 48, 16), 48), :] = rows.astype(bf16)
        return carry

    lax.fori_loop(0, NZ, gather, 0)
    loads[2].wait()
    da[...] = lax.dot_general(cot[...], wfull[...], (((1,), (1,)), ((), ())), preferred_element_type=f32)

    @tiles
    def _(c):
        at = lanes_of(c)
        d_pre = da[:, at] * fac[c]
        fac[c] = d_pre
        b1[g, :, at] = jnp.concatenate(
            [jnp.sum(d_pre, 0, keepdims=True), jnp.sum(d_pre * conv[c], 0, keepdims=True)], 0)

    b_done = exchange(b1, g, on_g)

    own_cols = pl.ds(pl.multiple_of(core * HALF, LANES), HALF)
    sib_cols = pl.ds(pl.multiple_of(sib * HALF, LANES), HALF)

    @tiles
    def _(c):
        rows = pl.ds(pl.multiple_of(c * LANES, LANES), LANES)
        a = act[:, lanes_of(c)]
        dims = (((0,), (0,)), ((), ()))
        gsend[rows, :] = lax.dot_general(a, cot[:, sib_cols], dims, preferred_element_type=f32).astype(bf16)
        gown[rows, :] = lax.dot_general(a, cot[:, own_cols], dims, preferred_element_type=f32)

    gc = rsems(1)
    send(gsend, grc, gc, sibling)

    b_done()
    b2[y] = summed(b1)
    b_done = exchange(b2, y, on_y)

    out[...] = jnp.dot(act[...], wfull[...], preferred_element_type=f32).astype(bf16)
    store_out = pltpu.make_async_copy(out, out_hbm, lsem.at[4])
    store_out.start()

    arrived(grc, gc)

    def add_core(j, carry):
        rows = pl.ds(pl.multiple_of(j * 192, 16), 192)
        t = gown[rows, :] + grc[rows, :].astype(f32)
        gown[rows, :] = t
        gxs[j] = t.astype(bf16)
        return carry

    lax.fori_loop(0, NX, add_core, 0)
    gx = rsems(4)
    for d in range(1, 4):
        j = rem(x + d, 4)
        send(gxs.at[j], gxr.at[d], gx + d, on_x(j))

    b_done()
    b3[z] = summed(b2)
    b_done = exchange(b3, z, on_z)
    b_done()
    sums = summed(b3)
    gb_ref[...] = sums[0:1] * stat[3:4]
    gn_ref[...] = sums[1:2] * stat[3:4]
    stat[4:5] = sums[0:1] * stat[2:3]
    stat[5:6] = sums[1:2] * stat[2:3]

    @tiles
    def _(c):
        at = lanes_of(c)
        d = (live() * (gain_ref[0:1, at] * stat[1:2, at])
             * (fac[c] - stat[4:5, at] - conv[c] * stat[5:6, at])).astype(bf16)
        ds_[0, :, at] = d[:REACH]
        ds_[1, :, at] = d[ROWS - REACH:]
        dwide[c, pl.ds(REACH, ROWS), :] = d.astype(f32)

    halo_done = halo(ds_, dr_)

    @tiles
    def _(c):
        at = lanes_of(c)
        d = dwide[c, pl.ds(REACH, ROWS), :]
        for k in range(TAPS):
            kt[k // 4, pl.ds(k % 4, 1), at] = jnp.sum(d * unit[c, pl.ds(k + 1, ROWS), :], 0, keepdims=True)
        kt[7, 3:4, at] = jnp.zeros((1, LANES), f32)

    k1 = rsems(8)
    for d in range(1, 8):
        j = rem(g + d, 8)
        send(kt.at[j], kr.at[d], k1 + d, on_g(j))

    for d in range(1, 4):
        arrived(gxr.at[d], gx + d)
    t = gown[pl.ds(pl.multiple_of(x * 192, 16), 192), :]
    for d in range(1, 4):
        t = t + gxr[d].astype(f32)
    t = t.reshape(24, 8, HALF)
    gyf[...] = t
    gys[...] = t.astype(bf16)
    gy = rsems(8)
    for d in range(1, 8):
        j = rem(y + d, 8)
        send(gys.at[pl.ds(rem(j, 2) * 12 + div(j, 2) * 3, 3)], gyr.at[d], gy + d, on_y(j))

    halo_done()

    @tiles
    def _(c):
        at = lanes_of(c)
        dwide[c, pl.ds(0, REACH), :] = dr_[0, :, at].astype(f32)
        dwide[c, pl.ds(REACH + ROWS, REACH), :] = dr_[1, :, at].astype(f32)
        acc = jnp.zeros((ROWS, LANES), f32)
        for k in range(TAPS):
            acc = acc + kern[pl.ds(k, 1), at] * dwide[c, pl.ds(TAPS - k, ROWS), :]
        v = glu[:, at].astype(f32)
        sg = jax.nn.sigmoid(glu[:, lanes_of(c, CH)].astype(f32))
        du = live() * acc * sg
        gg[:, at] = du.astype(bf16)
        gg[:, lanes_of(c, CH)] = (du * v * (1.0 - sg)).astype(bf16)

    store_gg = pltpu.make_async_copy(gg, gg_hbm, lsem.at[5])
    store_gg.start()

    for d in range(1, 8):
        arrived(kr.at[d], k1 + d)
    t = kt[g]
    for d in range(1, 8):
        t = t + kr[d]
    k2[y] = t
    k_done = exchange(k2, y, on_y)

    for d in range(1, 8):
        arrived(gyr.at[d], gy + d)
    t = gyf[pl.ds(yl * 12 + yh * 3, 3)]
    for d in range(1, 8):
        t = t + gyr[d].astype(f32)
    gz[...] = t
    owner = 2 * x + yl
    gzb = rsems(8)
    slot = rem(z + 8 - owner, 8)
    to_owner = copy(gz, gzr.at[slot], gzb + slot, on_z(owner))

    @pl.when(z != owner)
    def _():
        to_owner.start()

    k_done()
    k3[z] = summed(k2)
    k_done = exchange(k3, z, on_z)

    fbb = rsems(2)
    spread = []
    for d in range(1, 16):
        e = rem(core + d, 2)
        c_ = rem(ctx + d // 2, 8)
        spread.append(copy(fin.at[pl.ds(e, 2)], fb.at[core], fbb + core, (div(dp, 2) * 2 + e, c_)))

    @pl.when(z == owner)
    def _():
        t = gz[...]
        for d in range(1, 8):
            arrived(gzr.at[d], gzb + d)
            t = t + gzr[d]
        fin[...] = t * stat[3:4, 0:HALF].reshape(1, 1, HALF)
        for c in spread:
            c.start()
        fb[core] = fin[pl.ds(core, 2)]

    k_done()
    kf[g] = summed(k3) * stat[3:4]
    k_done = exchange(kf, g, on_g)
    k_done()
    for j in range(8):
        w = 4 if j < 7 else 3
        gk_ref[pl.ds(4 * j, w), :] = kf[j, 0:w, :]

    @pl.when(z != owner)
    def _():
        arrived(fb.at[core], fbb + core)

    arrived(fb.at[sib], fbb + sib)
    for h in range(2):
        v = fb[h].reshape(16, HALF)
        gp_ref[:, pl.ds(h * HALF, HALF)] = jnp.where(core == 0, v[0:BLOCK], v[16 - BLOCK:16])

    for c in pending:
        c.wait_send()

    @pl.when(yh == x)
    def _():
        for c in w1_sends:
            c.wait_send()

    @pl.when(z != owner)
    def _():
        to_owner.wait_send()

    @pl.when(z == owner)
    def _():
        for c in spread:
            c.wait_send()

    store_out.wait()
    store_gg.wait()


def body(glu_in, lengths, kernel, bn_gain, bn_bias, proj_weight, cotangent):
    vm = pltpu.VMEM
    anyspec = pl.BlockSpec(memory_space=pl.ANY)
    vspec = pl.BlockSpec(memory_space=pltpu.VMEM)
    sspec = pl.BlockSpec(memory_space=pltpu.SMEM)
    scratch = [
        vm((ROWS, 2 * CH), bf16), vm((ROWS, CH), bf16), vm((TAPS, CH), f32),
        vm((TILES, ROWS + 2 * REACH, LANES), f32), vm((TILES, ROWS, LANES), f32),
        vm((TILES, ROWS, LANES), f32), vm((TILES, ROWS + 2 * REACH, LANES), f32),
        vm((ROWS, CH), f32), vm((ROWS, CH), bf16), vm((ROWS, CH), bf16), vm((ROWS, 2 * CH), bf16),
        vm((NZ, NYH, NC, BLOCK, CH), bf16), vm((CH, CH), bf16),
        vm((2, REACH, CH), bf16), vm((2, REACH, CH), bf16), vm((2, REACH, CH), bf16), vm((2, REACH, CH), bf16),
        vm((8, 4, CH), f32), vm((8, 4, CH), f32), vm((8, 4, CH), f32),
        vm((8, 2, CH), f32), vm((8, 2, CH), f32), vm((8, 2, CH), f32),
        vm((8, CH), f32),
        vm((8, 4, CH), f32), vm((8, 4, CH), f32), vm((8, 4, CH), f32), vm((8, 4, CH), f32), vm((8, 4, CH), f32),
        vm((CH, HALF), f32), vm((CH, HALF), bf16), vm((CH, HALF), bf16),
        vm((NX, 192, HALF), bf16), vm((NX, 192, HALF), bf16),
        vm((24, 8, HALF), f32), vm((24, 8, HALF), bf16), vm((8, 3, 8, HALF), bf16),
        vm((3, 8, HALF), f32), vm((8, 3, 8, HALF), f32), vm((3, 8, HALF), f32), vm((2, 2, 8, HALF), f32),
        pltpu.SemaphoreType.DMA((160,)), pltpu.SemaphoreType.DMA((160,)), pltpu.SemaphoreType.DMA((6,)),
    ]
    outs = [
        jax.ShapeDtypeStruct((ROWS, CH), bf16),
        jax.ShapeDtypeStruct((ROWS, 2 * CH), bf16),
        jax.ShapeDtypeStruct((BLOCK, CH), f32),
        jax.ShapeDtypeStruct((TAPS, CH), f32),
        jax.ShapeDtypeStruct((1, CH), f32),
        jax.ShapeDtypeStruct((1, CH), f32),
    ]
    result, grad_glu, grad_proj, grad_kernel, grad_gain, grad_bias = pl.pallas_call(
        fused,
        out_shape=outs,
        in_specs=[anyspec, sspec, anyspec, vspec, vspec, anyspec, anyspec],
        out_specs=[anyspec, anyspec, vspec, vspec, vspec, vspec],
        scratch_shapes=scratch,
        compiler_params=pltpu.CompilerParams(
            collective_id=0, has_side_effects=True, vmem_limit_bytes=48 * 1024 * 1024),
        name="conformer_conv",
    )(glu_in[0], lengths, kernel, bn_gain[None], bn_bias[None], proj_weight, cotangent[0])
    return (result[None], grad_glu[None], grad_proj, grad_kernel, grad_gain[0], grad_bias[0])


def solution(mesh):
    in_specs = (P("dp", "ctx", None), P("dp"), P(), P(), P(), P("dp", None), P("dp", "ctx", None))
    out_specs = (P("dp", "ctx", None), P("dp", "ctx", None), P("dp", None), P(), P(), P())
    return jax.shard_map(body, mesh=mesh, in_specs=in_specs, out_specs=out_specs, check_vma=False)
```

time: 909 us -> 83.6 us (0.09)
  blocking collectives: 459 us -> 0 us
  waiting for transfers between devices: 337 us -> 0 us
  Pallas kernels: 0 us -> 73.8 us
  starting transfers between devices: 63.6 us -> 0 us
  between operations: 18.8 us -> 1.33 us
  other arithmetic: 14.3 us -> 1.21 us
    psum x2 -> x0, waiting for transfers between devices: 336 us -> none  [the longest x1 256 us: body(): kernel_sum = lax.psum(terms, ('dp', 'ctx'))]
    psum x3 -> x0, blocking collectives: 299 us -> none  [the longest x1 107 us: body(): lax.psum((jnp.sum(live * conv, 0), jnp.sum(live)), ('dp', 'ctx'))]
    unnamed x1 -> x0, blocking collectives: 160 us -> none
    pallas_call x0 -> x1, Pallas kernels: none -> 73.8 us  [body(): pl.pallas_call(fused, out_shape=outs, in_specs=[anyspec, sspec, anyspec,...]
    unnamed x16 -> x0, starting transfers between devices: 55.3 us -> none
  transfers between devices with their start and end apart: 23 -> 0, of which waited for: 3 -> 0; matrix products, arithmetic and copies ran while one was open for 19% -> 0% of each run, Pallas kernels for 0% -> 0%
where the time goes in v1:
time: 83.6 us; the launch traced here: 83.2 us
  Pallas kernels  73.8 us (88%)
  local copies, waits for them, and re-layouts  6.91 us (8%)
  between operations  1.33 us (2%)
  other arithmetic  1.21 us (1%)
    pallas_call x1, Pallas kernels, body(): pl.pallas_call(fused, out_shape=outs, in_specs=[anyspec, sspec, anyspec,...  73.8 us
    unnamed x16, local copies, waits for them, and re-layouts  6.9 us

profile of v1, /device:TPU:1, one launch (start us, length us, event | category | flops | bytes accessed | tf_op | source)
XLA Modules:
  0.0 83.2 jit_solution(932186170610806599)
XLA Ops:
  0.6 0.0 copy-start.4
  1.3 0.0 copy-start.5
  1.3 0.0 copy-done.4
  1.3 0.7 copy-done.5
  2.0 0.0 copy-start
  2.0 1.0 %copy-done = bf16[1,128,1536]{2,1,0:T(8,128)(2,1)S(1)} copy-done((bf16[1,128,1536]{2,1,0:T(8,128)(2,1)S(1)}, bf16[1,128,1536]{2,1,0:T(8,128)(2,1)}, u32[]{:S(2)}) %copy-start) | copy-done | bytes 393240
  3.0 0.0 copy-start.1
  3.0 0.9 %copy-done.1 = bf16[1,128,768]{2,1,0:T(8,128)(2,1)S(1)} copy-done((bf16[1,128,768]{2,1,0:T(8,128)(2,1)S(1)}, bf16[1,128,768]{2,1,0:T(8,128)(2,1)}, u32[]{:S(2)}) %copy-start.1) | copy-done | bytes 196632
  3.9 0.0 copy-start.2
  3.9 0.9 %copy-done.2 = f32[31,768]{1,0:T(8,128)S(1)} copy-done((f32[31,768]{1,0:T(8,128)S(1)}, f32[31,768]{1,0:T(8,128)}, u32[]{:S(2)}) %copy-start.2) | copy-done | bytes 95256
  4.8 0.0 copy-start.3
  4.8 0.7 copy-done.3
  5.5 73.8 %conformer_conv.1 = (bf16[128,768]{1,0:T(8,128)(2,1)S(1)}, bf16[128,1536]{1,0:T(8,128)(2,1)S(1)}, f32[12,768]{1,0:T(8,128)S(1)}, f32[31,768]{1,0:T(8,128)S(1)}, ...) custom-call(bf16[128,1536]{1,0:T(8,128)(2,1)S(1)} %bitcast.4, s32[1]{0:T(128)S(6)} %copy.17.len_ref, f32[31,768]{1,0:T(8,128)S(1)} %copy-done.2, ...), custom_call_target="tpu_custom_call" | custom-call | tf_op jit(solution)/shard_map/conformer_conv/pallas_call | solution.py:516
  79.4 0.6 reduce
  80.0 0.6 reduce.1
  80.6 0.7 copy.18
  81.2 0.7 copy.19
  82.0 0.6 copy.20
  82.6 0.6 copy.21
  (2 shorter events, 0.0 us)
Async XLA Ops:
  0.6 0.7 copy-start.4
  1.3 0.7 copy-start.5
  2.0 1.0 %copy-start = (bf16[1,128,1536]{2,1,0:T(8,128)(2,1)S(1)}, bf16[1,128,1536]{2,1,0:T(8,128)(2,1)}, u32[]{:S(2)}) copy-start(bf16[1,128,1536]{2,1,0:T(8,128)(2,1)} %param.7) | copy-start | bytes 1179652
  3.0 0.9 %copy-start.1 = (bf16[1,128,768]{2,1,0:T(8,128)(2,1)S(1)}, bf16[1,128,768]{2,1,0:T(8,128)(2,1)}, u32[]{:S(2)}) copy-start(bf16[1,128,768]{2,1,0:T(8,128)(2,1)} %param.13) | copy-start | bytes 589828
  3.9 0.9 %copy-start.2 = (f32[31,768]{1,0:T(8,128)S(1)}, f32[31,768]{1,0:T(8,128)}, u32[]{:S(2)}) copy-start(f32[31,768]{1,0:T(8,128)} %kern_hbm.1) | copy-start | bytes 285700
  4.8 0.7 copy-start.3

commit v2 on v1

--- a/solution.py
+++ b/solution.py
@@ -39,12 +39,12 @@
     lax.fori_loop(0, TILES, step, 0)
 
 
-def fused(glu_hbm, len_ref, kern_hbm, gain_ref, bias_ref, w_hbm, cot_hbm,
+def fused(glu_hbm, len_ref, kern_hbm, gain_in, bias_in, w_hbm, cot_hbm,
           out_hbm, gg_hbm, gp_ref, gk_ref, gn_ref, gb_ref,
           glu, cot, kern, unit, conv, fac, dwide, da, act, out, gg,
           wblk, wfull, hs, hr, ds_, dr_, a1, a2, a3, b1, b2, b3, stat,
           kt, kr, k2, k3, kf, gown, gsend, grc, gxs, gxr, gyf, gys, gyr, gz, gzr, fin, fb,
-          ssem, rsem, lsem):
+          gain_v, bias_v, ssem, rsem, lsem):
     dp = lax.axis_index("dp")
     ctx = lax.axis_index("ctx")
     z, yh, core = div(dp, 8), rem(div(dp, 2), 4), rem(dp, 2)
@@ -72,6 +72,7 @@
     sends = [0]
     recvs = [0]
     pending = []
+    cond = []
 
     def rsems(n):
         recvs[0] += n
@@ -93,6 +94,15 @@
             src_ref=dst, dst_ref=dst, send_sem=ssem.at[0], recv_sem=rsem.at[recv],
             device_id=sibling, device_id_type=pl.DeviceIdType.MESH).wait_recv()
 
+    def finish():
+        for c in pending:
+            c.wait_send()
+        for when, copies in cond:
+            @pl.when(when)
+            def _():
+                for c in copies:
+                    c.wait_send()
+
     def exchange(buf, me, where, n=8):
         base = rsems(n)
         for d in range(1, n):
@@ -105,10 +115,10 @@
         return done
 
     loads = [pltpu.make_async_copy(a, b, lsem.at[i]) for i, (a, b) in enumerate(
-        [(glu_hbm, glu), (kern_hbm, kern), (cot_hbm, cot)])]
+        [(glu_hbm, glu), (kern_hbm, kern), (cot_hbm, cot), (gain_in, gain_v), (bias_in, bias_v)])]
     for c in loads:
         c.start()
-    load_w = pltpu.make_async_copy(w_hbm, wblk.at[z, x, core], lsem.at[3])
+    load_w = pltpu.make_async_copy(w_hbm, wblk.at[z, x, core], lsem.at[5])
 
     @pl.when(yh == x)
     def _():
@@ -185,6 +195,8 @@
     mine = wblk.at[z, x, core]
     w1_sends = [copy(mine, mine, w1, on_y(rem(yh + d, 4) * 2 + yl)) for d in range(1, 4)]
 
+    cond.append((yh == x, w1_sends))
+
     @pl.when(yh == x)
     def _():
         load_w.wait()
@@ -200,7 +212,10 @@
         send(mine, mine, w2 + d, on_z(rem(z + d, 8)))
 
     halo_done()
-    loads[1].wait()
+    for c in (loads[1], loads[3], loads[4]):
+        c.wait()
+    stat[6:7] = gain_v[...].reshape(1, CH)
+    stat[7:8] = bias_v[...].reshape(1, CH)
 
     @tiles
     def _(c):
@@ -267,7 +282,7 @@
         at = lanes_of(c)
         normed = (conv[c] - stat[0:1, at]) * stat[1:2, at]
         conv[c] = normed
-        pre = gain_ref[0:1, at] * normed + bias_ref[0:1, at]
+        pre = stat[6:7, at] * normed + stat[7:8, at]
         sp = jax.nn.sigmoid(pre)
         m = live()
         act[:, at] = (m * pre * sp).astype(bf16)
@@ -316,7 +331,7 @@
     b_done = exchange(b2, y, on_y)
 
     out[...] = jnp.dot(act[...], wfull[...], preferred_element_type=f32).astype(bf16)
-    store_out = pltpu.make_async_copy(out, out_hbm, lsem.at[4])
+    store_out = pltpu.make_async_copy(out, out_hbm, lsem.at[6])
     store_out.start()
 
     arrived(grc, gc)
@@ -339,15 +354,15 @@
     b_done = exchange(b3, z, on_z)
     b_done()
     sums = summed(b3)
-    gb_ref[...] = sums[0:1] * stat[3:4]
-    gn_ref[...] = sums[1:2] * stat[3:4]
+    gb_ref[...] = (sums[0:1] * stat[3:4]).reshape(CH)
+    gn_ref[...] = (sums[1:2] * stat[3:4]).reshape(CH)
     stat[4:5] = sums[0:1] * stat[2:3]
     stat[5:6] = sums[1:2] * stat[2:3]
 
     @tiles
     def _(c):
         at = lanes_of(c)
-        d = (live() * (gain_ref[0:1, at] * stat[1:2, at])
+        d = (live() * (stat[6:7, at] * stat[1:2, at])
              * (fac[c] - stat[4:5, at] - conv[c] * stat[5:6, at])).astype(bf16)
         ds_[0, :, at] = d[:REACH]
         ds_[1, :, at] = d[ROWS - REACH:]
@@ -397,7 +412,7 @@
         gg[:, at] = du.astype(bf16)
         gg[:, lanes_of(c, CH)] = (du * v * (1.0 - sg)).astype(bf16)
 
-    store_gg = pltpu.make_async_copy(gg, gg_hbm, lsem.at[5])
+    store_gg = pltpu.make_async_copy(gg, gg_hbm, lsem.at[7])
     store_gg.start()
 
     for d in range(1, 8):
@@ -419,6 +434,8 @@
     slot = rem(z + 8 - owner, 8)
     to_owner = copy(gz, gzr.at[slot], gzb + slot, on_z(owner))
 
+    cond.append((z != owner, [to_owner]))
+
     @pl.when(z != owner)
     def _():
         to_owner.start()
@@ -433,6 +450,8 @@
         e = rem(core + d, 2)
         c_ = rem(ctx + d // 2, 8)
         spread.append(copy(fin.at[pl.ds(e, 2)], fb.at[core], fbb + core, (div(dp, 2) * 2 + e, c_)))
+
+    cond.append((z == owner, spread))
 
     @pl.when(z == owner)
     def _():
@@ -462,29 +481,23 @@
         v = fb[h].reshape(16, HALF)
         gp_ref[:, pl.ds(h * HALF, HALF)] = jnp.where(core == 0, v[0:BLOCK], v[16 - BLOCK:16])
 
-    for c in pending:
-        c.wait_send()
-
-    @pl.when(yh == x)
-    def _():
-        for c in w1_sends:
-            c.wait_send()
-
-    @pl.when(z != owner)
-    def _():
-        to_owner.wait_send()
-
-    @pl.when(z == owner)
-    def _():
-        for c in spread:
-            c.wait_send()
-
+    finish()
     store_out.wait()
     store_gg.wait()
 
 
+def handed_on(*refs):
+    sem = refs[12]
+    copies = [pltpu.make_async_copy(refs[i], refs[6 + i], sem.at[i]) for i in range(6)]
+    for c in copies:
+        c.start()
+    for c in copies:
+        c.wait()
+
+
 def body(glu_in, lengths, kernel, bn_gain, bn_bias, proj_weight, cotangent):
     vm = pltpu.VMEM
+    hbm = functools.partial(pltpu.with_memory_space_constraint, memory_space=pltpu.HBM)
     anyspec = pl.BlockSpec(memory_space=pl.ANY)
     vspec = pl.BlockSpec(memory_space=pltpu.VMEM)
     sspec = pl.BlockSpec(memory_space=pltpu.SMEM)
@@ -503,27 +516,37 @@
         vm((NX, 192, HALF), bf16), vm((NX, 192, HALF), bf16),
         vm((24, 8, HALF), f32), vm((24, 8, HALF), bf16), vm((8, 3, 8, HALF), bf16),
         vm((3, 8, HALF), f32), vm((8, 3, 8, HALF), f32), vm((3, 8, HALF), f32), vm((2, 2, 8, HALF), f32),
-        pltpu.SemaphoreType.DMA((160,)), pltpu.SemaphoreType.DMA((160,)), pltpu.SemaphoreType.DMA((6,)),
+        vm((CH,), f32), vm((CH,), f32),
+        pltpu.SemaphoreType.DMA((160,)), pltpu.SemaphoreType.DMA((160,)), pltpu.SemaphoreType.DMA((8,)),
     ]
     outs = [
         jax.ShapeDtypeStruct((ROWS, CH), bf16),
         jax.ShapeDtypeStruct((ROWS, 2 * CH), bf16),
         jax.ShapeDtypeStruct((BLOCK, CH), f32),
         jax.ShapeDtypeStruct((TAPS, CH), f32),
-        jax.ShapeDtypeStruct((1, CH), f32),
-        jax.ShapeDtypeStruct((1, CH), f32),
+        jax.ShapeDtypeStruct((CH,), f32),
+        jax.ShapeDtypeStruct((CH,), f32),
     ]
-    result, grad_glu, grad_proj, grad_kernel, grad_gain, grad_bias = pl.pallas_call(
+    results = pl.pallas_call(
         fused,
         out_shape=outs,
-        in_specs=[anyspec, sspec, anyspec, vspec, vspec, anyspec, anyspec],
+        in_specs=[anyspec, sspec, anyspec, anyspec, anyspec, anyspec, anyspec],
         out_specs=[anyspec, anyspec, vspec, vspec, vspec, vspec],
         scratch_shapes=scratch,
         compiler_params=pltpu.CompilerParams(
-            collective_id=0, has_side_effects=True, vmem_limit_bytes=48 * 1024 * 1024),
+            collective_id=0, has_side_effects=True, vmem_limit_bytes=40 * 1024 * 1024),
         name="conformer_conv",
-    )(glu_in[0], lengths, kernel, bn_gain[None], bn_bias[None], proj_weight, cotangent[0])
-    return (result[None], grad_glu[None], grad_proj, grad_kernel, grad_gain[0], grad_bias[0])
+    )(hbm(glu_in[0]), lengths, hbm(kernel), hbm(bn_gain), hbm(bn_bias), hbm(proj_weight), hbm(cotangent[0]))
+    result, grad_glu, grad_proj, grad_kernel, grad_gain, grad_bias = pl.pallas_call(
+        handed_on,
+        out_shape=outs,
+        in_specs=[anyspec] * 6,
+        out_specs=[anyspec] * 6,
+        scratch_shapes=[pltpu.SemaphoreType.DMA((6,))],
+        compiler_params=pltpu.CompilerParams(vmem_limit_bytes=1024 * 1024),
+        name="handed_on",
+    )(*results)
+    return (result[None], grad_glu[None], grad_proj, grad_kernel, grad_gain, grad_bias)
 
 
 def solution(mesh):

time: 83.6 us -> 75.5 us (0.903)
  local copies, waits for them, and re-layouts: 6.91 us -> 0 us
  other arithmetic: 1.21 us -> 0 us
    unnamed x16 -> x0, local copies, waits for them, and re-layouts: 6.9 us -> none
    pallas_call x2 -> x0, other arithmetic: 1.21 us -> none  [body(): pl.pallas_call(fused, out_shape=outs, in_specs=[anyspec, sspec, anyspec,...]
    pallas_call x0 -> x1, Pallas kernels: none -> 0.91 us  [body(): pl.pallas_call(handed_on, out_shape=outs, in_specs=[anyspec] * 6, out_spe...]
where the time goes in v2:
time: 75.5 us; the launch traced here: 75.4 us
  Pallas kernels  74.1 us (98%)
  between operations  1.29 us (2%)
    pallas_call x1, Pallas kernels, body(): pl.pallas_call(fused, out_shape=outs, in_specs=[anyspec, sspec, anyspec,...  73.2 us

profile of v2, /device:TPU:1, one launch (start us, length us, event | category | flops | bytes accessed | tf_op | source)
XLA Modules:
  0.0 75.4 jit_solution(3897236525963892524)
XLA Ops:
  1.3 73.2 %conformer_conv.1 = (bf16[128,768]{1,0:T(8,128)(2,1)S(1)}, bf16[128,1536]{1,0:T(8,128)(2,1)S(1)}, f32[12,768]{1,0:T(8,128)S(1)}, f32[31,768]{1,0:T(8,128)S(1)}, f32[768]{0:T(1024)S(1)}, /*index=5*/f32[768]{0:T(1024)S(1)}) custom-call(bf16[128,1536]{1,0:T(8,128)(2,1)} %bitcast.4, s32[1]{0:T(128)S(6)} %copy.13.len_ref, f32[31,768]{1,0:T(8,128)} %kern_hbm.1, ...), custom_call_target="tpu_custom_call" | custom-call | tf_op jit(solution)/shard_map/conformer_conv/pallas_call | solution.py:530
  74.5 0.9 %handed_on.1 = (bf16[128,768]{1,0:T(8,128)(2,1)}, bf16[128,1536]{1,0:T(8,128)(2,1)}, f32[12,768]{1,0:T(8,128)}, f32[31,768]{1,0:T(8,128)}, f32[768]{0:T(1024)}, /*index=5*/f32[768]{0:T(1024)}) custom-call(bf16[128,768]{1,0:T(8,128)(2,1)S(1)} %get-tuple-element.18.refs_0_, bf16[128,1536]{1,0:T(8,128)(2,1)S(1)} %get-tuple-element.19.refs_1_, ...), custom_call_target="tpu_custom_call" | custom-call | tf_op jit(solution)/shard_map/handed_on/pallas_call | solution.py:540

commit v3 on v2

--- a/solution.py
+++ b/solution.py
@@ -17,6 +17,8 @@
 HALF = CH // 2
 REACH = 16
 BLOCK = CH // (NZ * NYH * NC)
+CHUNKS = HALF // LANES
+NEAR = (0, 1, 7, 2, 6, 3, 5, 4)
 
 
 def rem(a, b):
@@ -41,9 +43,9 @@
 
 def fused(glu_hbm, len_ref, kern_hbm, gain_in, bias_in, w_hbm, cot_hbm,
           out_hbm, gg_hbm, gp_ref, gk_ref, gn_ref, gb_ref,
-          glu, cot, kern, unit, conv, fac, dwide, da, act, out, gg,
-          wblk, wfull, hs, hr, ds_, dr_, a1, a2, a3, b1, b2, b3, stat,
-          kt, kr, k2, k3, kf, gown, gsend, grc, gxs, gxr, gyf, gys, gyr, gz, gzr, fin, fb,
+          glu, cot, kern, unit, conv, fac, dwide, da, act, out, gg, ub,
+          wl, wr, wb, wfull, hs, hr, ds_, dr_, a1, a2, a3, b1, b2, b3, stat,
+          kt, kr, k2, k3, kf, uq, ur, u2, gown, gsend, grc, gxs, gxr, gyf, gys, gyr, gz, gzr, fin, fb,
           gain_v, bias_v, ssem, rsem, lsem):
     dp = lax.axis_index("dp")
     ctx = lax.axis_index("ctx")
@@ -114,31 +116,65 @@
 
         return done
 
-    loads = [pltpu.make_async_copy(a, b, lsem.at[i]) for i, (a, b) in enumerate(
-        [(glu_hbm, glu), (kern_hbm, kern), (cot_hbm, cot), (gain_in, gain_v), (bias_in, bias_v)])]
-    for c in loads:
-        c.start()
-    load_w = pltpu.make_async_copy(w_hbm, wblk.at[z, x, core], lsem.at[5])
-
-    @pl.when(yh == x)
-    def _():
-        load_w.start()
-
     barrier = pltpu.get_barrier_semaphore()
     peers = [on_g(rem(g + d, 8)) for d in range(1, 8)]
     peers += [on_y(rem(y + d, 8)) for d in range(1, 8)]
     peers += [on_z(rem(z + d, 8)) for d in range(1, 8)]
     flip = yh * 2 + (1 - yl)
+    peers += [dev(z, rem(y + 2 * d, 8), x, sib) for d in range(1, 4)]
     peers += [dev(z, flip, div(rem(g + d, 8), 2), rem(rem(g + d, 8), 2)) for d in range(1, 8)]
     for p in peers:
         pl.semaphore_signal(barrier, inc=1, device_id=p, device_id_type=pl.DeviceIdType.MESH)
 
+    loads = [pltpu.make_async_copy(a, b, lsem.at[i]) for i, (a, b) in enumerate(
+        [(glu_hbm, glu), (kern_hbm, kern), (cot_hbm, cot), (gain_in, gain_v), (bias_in, bias_v)])]
+    load_w = pltpu.make_async_copy(w_hbm, wl, lsem.at[5])
+
+    @pl.when(yh == x)
+    def _():
+        load_w.start()
+
+    for c in loads:
+        c.start()
+
     pos0 = ctx * ROWS
     length = len_ref[0]
     n_live = jnp.clip(length - pos0, 0, ROWS).astype(f32)
 
     def live():
         return (lax.broadcasted_iota(jnp.int32, (ROWS, LANES), 0) + pos0 < length).astype(f32)
+
+    pl.semaphore_wait(barrier, len(peers))
+
+    own_cols = pl.ds(pl.multiple_of(core * HALF, LANES), HALF)
+    sib_cols = pl.ds(pl.multiple_of(sib * HALF, LANES), HALF)
+    w1, w2, w3, w4 = rsems(2), rsems(8), rsems(8), rsems(8)
+    mine = wb.at[core, x, 0]
+    w1_sends = [copy(wl.at[:, sib_cols], wr.at[core], w1 + core, sibling)]
+    for d in range(1, 4):
+        y_ = rem(yh + d, 4) * 2 + yl
+        w1_sends.append(copy(wl.at[:, own_cols], wr.at[core], w1 + core, dev(z, y_, x, core)))
+        w1_sends.append(copy(wl.at[:, sib_cols], wr.at[core], w1 + core, dev(z, y_, x, sib)))
+    cond.append((yh == x, w1_sends))
+
+    @pl.when(yh == x)
+    def _():
+        load_w.wait()
+        for c in w1_sends:
+            c.start()
+        wr[core] = wl[:, own_cols]
+
+    def w1_done():
+        @pl.when(yh != x)
+        def _():
+            arrived(wr.at[core], w1 + core)
+
+        arrived(wr.at[sib], w1 + sib)
+        rows = jnp.concatenate([wr[0].astype(f32), wr[1].astype(f32)], 0)
+        wb[core, x, 0] = rows.reshape(3, 8, HALF).astype(bf16)
+        for d in range(1, 8):
+            p = NEAR.index(8 - d)
+            send(mine, wb.at[core, x, p], w2 + p, on_z(rem(z + d, 8)))
 
     loads[0].wait()
 
@@ -149,6 +185,7 @@
         u = (live() * v * sg).astype(bf16)
         hs[0, :, lanes_of(c)] = u[:REACH]
         hs[1, :, lanes_of(c)] = u[ROWS - REACH:]
+        ub[pl.ds(REACH, ROWS), lanes_of(c)] = u
         unit[c, pl.ds(REACH, ROWS), :] = u.astype(f32)
 
     @pl.when(ctx == 0)
@@ -161,7 +198,6 @@
         hr[1] = jnp.zeros((REACH, CH), bf16)
         dr_[1] = jnp.zeros((REACH, CH), bf16)
 
-    pl.semaphore_wait(barrier, len(peers))
 
     def halo(src, dst):
         base = rsems(2)
@@ -191,31 +227,13 @@
 
     halo_done = halo(hs, hr)
 
-    w1 = rsems(1)
-    mine = wblk.at[z, x, core]
-    w1_sends = [copy(mine, mine, w1, on_y(rem(yh + d, 4) * 2 + yl)) for d in range(1, 4)]
-
-    cond.append((yh == x, w1_sends))
-
-    @pl.when(yh == x)
-    def _():
-        load_w.wait()
-        for c in w1_sends:
-            c.start()
-
-    @pl.when(yh != x)
-    def _():
-        arrived(mine, w1)
-
-    w2 = rsems(8)
-    for d in range(1, 8):
-        send(mine, mine, w2 + d, on_z(rem(z + d, 8)))
-
     halo_done()
     for c in (loads[1], loads[3], loads[4]):
         c.wait()
     stat[6:7] = gain_v[...].reshape(1, CH)
     stat[7:8] = bias_v[...].reshape(1, CH)
+    ub[pl.ds(0, REACH), :] = hr[0]
+    ub[pl.ds(REACH + ROWS, REACH), :] = hr[1]
 
     @tiles
     def _(c):
@@ -229,19 +247,25 @@
         s = jnp.sum(m * acc, 0, keepdims=True)
         centred = acc - s / jnp.maximum(n_live, 1.0)
         q = jnp.sum(m * centred * centred, 0, keepdims=True)
-        n = jnp.full((1, LANES), n_live, f32)
-        a1[g, :, lanes_of(c)] = jnp.concatenate([s, q, n, jnp.zeros((1, LANES), f32)], 0)
+        a1[g, :, lanes_of(c)] = jnp.concatenate([s, q], 0)
+
+    a1[g, :, pl.ds(CH, LANES)] = jnp.full((2, LANES), n_live, f32)
 
     def merged(buf):
         total = buf[0]
         for i in range(1, 8):
             total = total + buf[i]
-        s, q, n = total[0:1], total[1:2], total[2:3]
-        mean = s / jnp.maximum(n, 1.0)
+        s, q, n = total[0:1, 0:CH], total[1:2, 0:CH], total[0:1, CH:]
+        mean = s / jnp.maximum(jnp.concatenate([n] * TILES, 1), 1.0)
         for i in range(8):
-            off = buf[i, 0:1, :] - buf[i, 2:3, :] * mean
-            q = q + off * off / jnp.maximum(buf[i, 2:3, :], 1.0)
+            n_i = buf[i, 0:1, CH:]
+            r_i = 1.0 / jnp.maximum(n_i, 1.0)
+            off = buf[i, 0:1, 0:CH] - jnp.concatenate([n_i] * TILES, 1) * mean
+            q = q + off * off * jnp.concatenate([r_i] * TILES, 1)
         return s, q, n
+
+    def packed(s, q, n):
+        return jnp.concatenate([jnp.concatenate([s, n], 1), jnp.concatenate([q, n], 1)], 0)
 
     def summed(buf):
         total = buf[0]
@@ -250,28 +274,56 @@
         return total
 
     a_done = exchange(a1, g, on_g)
-    for d in range(1, 8):
-        arrived(wblk.at[rem(z + (8 - d), 8), x, core], w2 + d)
-    w3 = rsems(4)
-    w4 = rsems(4)
-    strip = wblk.at[:, x, core]
-    for d in range(1, 4):
-        send(strip, strip, w3 + d, on_x(rem(x + d, 4)))
-    send(strip, strip, w4, sibling)
-
-    zero = jnp.zeros((1, CH), f32)
+
+    w1_done()
+
+    n_rows = jnp.clip(length - pos0, 0, ROWS)
+    tap = lax.broadcasted_iota(jnp.int32, (32, ROWS + 2 * REACH), 0)
+    row = lax.broadcasted_iota(jnp.int32, (32, ROWS + 2 * REACH), 1) - tap - 1
+    window = ((row >= 0) & (row < n_rows) & (tap < TAPS)).astype(f32).astype(bf16)
+    u_sum = jnp.dot(window, ub[...], preferred_element_type=f32)
+    for j in range(8):
+        uq[j, 0:4, :] = u_sum[4 * j:4 * j + 4]
+
+    @tiles
+    def _(c):
+        at = lanes_of(c)
+        d = live() * conv[c]
+        for k in range(TAPS):
+            uq[k // 4, pl.ds(4 + k % 4, 1), at] = jnp.sum(d * unit[c, pl.ds(k + 1, ROWS), :], 0, keepdims=True)
+        uq[7, 7:8, at] = jnp.zeros((1, LANES), f32)
+
     a_done()
-    a2[y] = jnp.concatenate([*merged(a1), zero], 0)
+    a2[y] = packed(*merged(a1))
     a_done = exchange(a2, y, on_y)
+
+    groups = ((0, 5), (5, 3))
+
+    def onward(i):
+        first, size = groups[i]
+        for p in range(max(first, 1), first + size):
+            arrived(wb.at[core, x, p], w2 + p)
+        strip = wb.at[core, x, pl.ds(first, size)]
+        for d in range(1, 4):
+            send(strip, strip, w3 + 4 * i + d, on_x(rem(x + d, 4)))
+        send(strip, strip, w4 + 4 * i, sibling)
+
+    def across(i):
+        first, size = groups[i]
+        for d in range(1, 4):
+            piece = wb.at[core, rem(x + (4 - d), 4), pl.ds(first, size)]
+            arrived(piece, w3 + 4 * i + d)
+            send(piece, piece, w4 + 4 * i + d, sibling)
+
+    onward(0)
     a_done()
-    a3[z] = jnp.concatenate([*merged(a2), zero], 0)
+    a3[z] = packed(*merged(a2))
     a_done = exchange(a3, z, on_z)
-    for d in range(1, 4):
-        piece = wblk.at[:, rem(x + (4 - d), 4), core]
-        arrived(piece, w3 + d)
-        send(piece, piece, w4 + d, sibling)
+    onward(1)
+    across(0)
     a_done()
     s, q, n = merged(a3)
+    n = jnp.concatenate([n] * TILES, 1)
     stat[0:1] = s / n
     stat[1:2] = lax.rsqrt(q / n + eps)
     stat[2:3] = 1.0 / n
@@ -288,19 +340,22 @@
         act[:, at] = (m * pre * sp).astype(bf16)
         fac[c] = m * sp * (1.0 + pre * (1.0 - sp))
 
-    for d in range(4):
-        arrived(wblk.at[:, rem(x + (4 - d), 4), sib], w4 + d)
-
-    def gather(i, carry):
-        for p in range(2):
-            rows = jnp.concatenate(
-                [wblk[i, 2 * p + h, e].astype(f32) for h in range(2) for e in range(2)], 0)
-            wfull[pl.ds(pl.multiple_of(i * 96 + p * 48, 16), 48), :] = rows.astype(bf16)
-        return carry
-
-    lax.fori_loop(0, NZ, gather, 0)
+    across(1)
+    uq1 = rsems(8)
+    for d in range(1, 8):
+        j = rem(g + d, 8)
+        send(uq.at[j], ur.at[d], uq1 + d, on_g(j))
+    for i, (first, size) in enumerate(groups):
+        for d in range(4):
+            arrived(wb.at[sib, rem(x + (4 - d), 4), pl.ds(first, size)], w4 + 4 * i + d)
+    for p in range(NZ):
+        rows = pl.ds(pl.multiple_of(rem(z + NEAR[p], 8) * 96, 16), 96)
+        for h in range(2):
+            wfull[h, rows, :] = wb[h, :, p].astype(f32).reshape(96, HALF).astype(bf16)
     loads[2].wait()
-    da[...] = lax.dot_general(cot[...], wfull[...], (((1,), (1,)), ((), ())), preferred_element_type=f32)
+    nt = (((1,), (1,)), ((), ()))
+    da[...] = (lax.dot_general(cot[:, 0:HALF], wfull[0], nt, preferred_element_type=f32)
+               + lax.dot_general(cot[:, HALF:CH], wfull[1], nt, preferred_element_type=f32))
 
     @tiles
     def _(c):
@@ -312,46 +367,80 @@
 
     b_done = exchange(b1, g, on_g)
 
-    own_cols = pl.ds(pl.multiple_of(core * HALF, LANES), HALF)
-    sib_cols = pl.ds(pl.multiple_of(sib * HALF, LANES), HALF)
-
-    @tiles
-    def _(c):
+    tn = (((0,), (0,)), ((), ()))
+
+    gc, gx, gy = rsems(CHUNKS), rsems(4 * CHUNKS), rsems(8 * CHUNKS)
+
+    @tiles
+    def _(c):
+        at = lanes_of(c)
         rows = pl.ds(pl.multiple_of(c * LANES, LANES), LANES)
-        a = act[:, lanes_of(c)]
-        dims = (((0,), (0,)), ((), ()))
-        gsend[rows, :] = lax.dot_general(a, cot[:, sib_cols], dims, preferred_element_type=f32).astype(bf16)
-        gown[rows, :] = lax.dot_general(a, cot[:, own_cols], dims, preferred_element_type=f32)
-
-    gc = rsems(1)
-    send(gsend, grc, gc, sibling)
-
+        a = act[:, at]
+        g_sib = lax.dot_general(a, cot[:, sib_cols], tn, preferred_element_type=f32).astype(bf16)
+        g_own = lax.dot_general(a, cot[:, own_cols], tn, preferred_element_type=f32)
+        for q in range(CHUNKS):
+            gsend[q, rows, :] = g_sib[:, q * LANES:(q + 1) * LANES]
+            gown[q, rows, :] = g_own[:, q * LANES:(q + 1) * LANES]
+        d = fac[c]
+        for k in range(TAPS):
+            kt[k // 4, pl.ds(k % 4, 1), at] = jnp.sum(d * unit[c, pl.ds(k + 1, ROWS), :], 0, keepdims=True)
+        kt[7, 3:4, at] = jnp.zeros((1, LANES), f32)
+
+    for q in range(CHUNKS):
+        send(gsend.at[q], grc.at[q], gc + q, sibling)
+    k1 = rsems(8)
+    for d in range(1, 8):
+        j = rem(g + d, 8)
+        send(kt.at[j], kr.at[d], k1 + d, on_g(j))
     b_done()
     b2[y] = summed(b1)
     b_done = exchange(b2, y, on_y)
-
-    out[...] = jnp.dot(act[...], wfull[...], preferred_element_type=f32).astype(bf16)
-    store_out = pltpu.make_async_copy(out, out_hbm, lsem.at[6])
-    store_out.start()
-
-    arrived(grc, gc)
-
-    def add_core(j, carry):
-        rows = pl.ds(pl.multiple_of(j * 192, 16), 192)
-        t = gown[rows, :] + grc[rows, :].astype(f32)
-        gown[rows, :] = t
-        gxs[j] = t.astype(bf16)
-        return carry
-
-    lax.fori_loop(0, NX, add_core, 0)
-    gx = rsems(4)
-    for d in range(1, 4):
-        j = rem(x + d, 4)
-        send(gxs.at[j], gxr.at[d], gx + d, on_x(j))
+    for d in range(1, 8):
+        arrived(ur.at[d], uq1 + d)
+    t = uq[g]
+    for d in range(1, 8):
+        t = t + ur[d]
+    u2[y] = t
+    u_done = exchange(u2, y, on_y)
+
+    for q in range(CHUNKS):
+        arrived(grc.at[q], gc + q)
+        t = gown[q] + grc[q].astype(f32)
+        gown[q] = t
+        gxs[q] = t.astype(bf16).reshape(NX, 192, LANES)
+        for d in range(1, 4):
+            j = rem(x + d, 4)
+            send(gxs.at[q, j], gxr.at[q, d], gx + 4 * q + d, on_x(j))
 
     b_done()
     b3[z] = summed(b2)
     b_done = exchange(b3, z, on_z)
+
+    def x_part(q):
+        for d in range(1, 4):
+            arrived(gxr.at[q, d], gx + 4 * q + d)
+        t = gown[q, pl.ds(pl.multiple_of(x * 192, 16), 192), :]
+        for d in range(1, 4):
+            t = t + gxr[q, d].astype(f32)
+        t = t.reshape(24, 8, LANES)
+        gyf[q] = t
+        gys[q] = t.astype(bf16)
+        for d in range(1, 8):
+            j = rem(y + d, 8)
+            send(gys.at[q, pl.ds(rem(j, 2) * 12 + div(j, 2) * 3, 3)], gyr.at[q, d], gy + 8 * q + d, on_y(j))
+
+    for d in range(1, 8):
+        arrived(kr.at[d], k1 + d)
+    t = kt[g]
+    for d in range(1, 8):
+        t = t + kr[d]
+    k2[y] = t
+    k_done = exchange(k2, y, on_y)
+    x_part(0)
+    for h in range(2):
+        out[:, h * HALF:(h + 1) * HALF] = jnp.dot(act[...], wfull[h], preferred_element_type=f32).astype(bf16)
+    store_out = pltpu.make_async_copy(out, out_hbm, lsem.at[6])
+    store_out.start()
     b_done()
     sums = summed(b3)
     gb_ref[...] = (sums[0:1] * stat[3:4]).reshape(CH)
@@ -370,31 +459,28 @@
 
     halo_done = halo(ds_, dr_)
 
-    @tiles
-    def _(c):
-        at = lanes_of(c)
-        d = dwide[c, pl.ds(REACH, ROWS), :]
-        for k in range(TAPS):
-            kt[k // 4, pl.ds(k % 4, 1), at] = jnp.sum(d * unit[c, pl.ds(k + 1, ROWS), :], 0, keepdims=True)
-        kt[7, 3:4, at] = jnp.zeros((1, LANES), f32)
-
-    k1 = rsems(8)
-    for d in range(1, 8):
-        j = rem(g + d, 8)
-        send(kt.at[j], kr.at[d], k1 + d, on_g(j))
-
-    for d in range(1, 4):
-        arrived(gxr.at[d], gx + d)
-    t = gown[pl.ds(pl.multiple_of(x * 192, 16), 192), :]
-    for d in range(1, 4):
-        t = t + gxr[d].astype(f32)
-    t = t.reshape(24, 8, HALF)
-    gyf[...] = t
-    gys[...] = t.astype(bf16)
-    gy = rsems(8)
-    for d in range(1, 8):
-        j = rem(y + d, 8)
-        send(gys.at[pl.ds(rem(j, 2) * 12 + div(j, 2) * 3, 3)], gyr.at[d], gy + d, on_y(j))
+    u_done()
+    u_all = summed(u2)
+    k_done()
+    u_rows, q_rows = u_all[0:4], u_all[4:8]
+    inv = stat[1:2]
+    k3[z] = (stat[6:7] * inv) * (
+        summed(k2) - stat[4:5] * u_rows - stat[5:6] * (inv * (q_rows - stat[0:1] * u_rows)))
+    k_done = exchange(k3, z, on_z)
+    x_part(1)
+    x_part(2)
+
+    owner = 2 * x + yl
+    gzb = rsems(8)
+    slot = rem(z + 8 - owner, 8)
+
+    def y_part(q):
+        for d in range(1, 8):
+            arrived(gyr.at[q, d], gy + 8 * q + d)
+        t = gyf[q, pl.ds(yl * 12 + yh * 3, 3)]
+        for d in range(1, 8):
+            t = t + gyr[q, d].astype(f32)
+        gz[q] = t
 
     halo_done()
 
@@ -415,25 +501,9 @@
     store_gg = pltpu.make_async_copy(gg, gg_hbm, lsem.at[7])
     store_gg.start()
 
-    for d in range(1, 8):
-        arrived(kr.at[d], k1 + d)
-    t = kt[g]
-    for d in range(1, 8):
-        t = t + kr[d]
-    k2[y] = t
-    k_done = exchange(k2, y, on_y)
-
-    for d in range(1, 8):
-        arrived(gyr.at[d], gy + d)
-    t = gyf[pl.ds(yl * 12 + yh * 3, 3)]
-    for d in range(1, 8):
-        t = t + gyr[d].astype(f32)
-    gz[...] = t
-    owner = 2 * x + yl
-    gzb = rsems(8)
-    slot = rem(z + 8 - owner, 8)
+    for q in range(CHUNKS):
+        y_part(q)
     to_owner = copy(gz, gzr.at[slot], gzb + slot, on_z(owner))
-
     cond.append((z != owner, [to_owner]))
 
     @pl.when(z != owner)
@@ -441,8 +511,8 @@
         to_owner.start()
 
     k_done()
-    k3[z] = summed(k2)
-    k_done = exchange(k3, z, on_z)
+    kf[g] = summed(k3) * stat[3:4]
+    k_done = exchange(kf, g, on_g)
 
     fbb = rsems(2)
     spread = []
@@ -450,23 +520,23 @@
         e = rem(core + d, 2)
         c_ = rem(ctx + d // 2, 8)
         spread.append(copy(fin.at[pl.ds(e, 2)], fb.at[core], fbb + core, (div(dp, 2) * 2 + e, c_)))
-
     cond.append((z == owner, spread))
 
     @pl.when(z == owner)
     def _():
-        t = gz[...]
         for d in range(1, 8):
             arrived(gzr.at[d], gzb + d)
-            t = t + gzr[d]
-        fin[...] = t * stat[3:4, 0:HALF].reshape(1, 1, HALF)
+        for q in range(CHUNKS):
+            t = gz[q]
+            for d in range(1, 8):
+                t = t + gzr[d, q]
+            t = t * stat[3:4, 0:LANES].reshape(1, 1, LANES)
+            for u in range(3):
+                fin[u, q] = t[u]
         for c in spread:
             c.start()
         fb[core] = fin[pl.ds(core, 2)]
 
-    k_done()
-    kf[g] = summed(k3) * stat[3:4]
-    k_done = exchange(kf, g, on_g)
     k_done()
     for j in range(8):
         w = 4 if j < 7 else 3
@@ -478,8 +548,9 @@
 
     arrived(fb.at[sib], fbb + sib)
     for h in range(2):
-        v = fb[h].reshape(16, HALF)
-        gp_ref[:, pl.ds(h * HALF, HALF)] = jnp.where(core == 0, v[0:BLOCK], v[16 - BLOCK:16])
+        for q in range(CHUNKS):
+            v = jnp.concatenate([fb[h, 0, q], fb[h, 1, q]], 0)
+            gp_ref[:, pl.ds(h * HALF + q * LANES, LANES)] = jnp.where(core == 0, v[0:BLOCK], v[16 - BLOCK:16])
 
     finish()
     store_out.wait()
@@ -506,18 +577,22 @@
         vm((TILES, ROWS + 2 * REACH, LANES), f32), vm((TILES, ROWS, LANES), f32),
         vm((TILES, ROWS, LANES), f32), vm((TILES, ROWS + 2 * REACH, LANES), f32),
         vm((ROWS, CH), f32), vm((ROWS, CH), bf16), vm((ROWS, CH), bf16), vm((ROWS, 2 * CH), bf16),
-        vm((NZ, NYH, NC, BLOCK, CH), bf16), vm((CH, CH), bf16),
+        vm((ROWS + 2 * REACH, CH), bf16),
+        vm((BLOCK, CH), bf16), vm((NC, BLOCK, HALF), bf16),
+        vm((NC, NYH, NZ, 3, 8, HALF), bf16), vm((NC, CH, HALF), bf16),
         vm((2, REACH, CH), bf16), vm((2, REACH, CH), bf16), vm((2, REACH, CH), bf16), vm((2, REACH, CH), bf16),
-        vm((8, 4, CH), f32), vm((8, 4, CH), f32), vm((8, 4, CH), f32),
+        vm((8, 2, CH + LANES), f32), vm((8, 2, CH + LANES), f32), vm((8, 2, CH + LANES), f32),
         vm((8, 2, CH), f32), vm((8, 2, CH), f32), vm((8, 2, CH), f32),
         vm((8, CH), f32),
         vm((8, 4, CH), f32), vm((8, 4, CH), f32), vm((8, 4, CH), f32), vm((8, 4, CH), f32), vm((8, 4, CH), f32),
-        vm((CH, HALF), f32), vm((CH, HALF), bf16), vm((CH, HALF), bf16),
-        vm((NX, 192, HALF), bf16), vm((NX, 192, HALF), bf16),
-        vm((24, 8, HALF), f32), vm((24, 8, HALF), bf16), vm((8, 3, 8, HALF), bf16),
-        vm((3, 8, HALF), f32), vm((8, 3, 8, HALF), f32), vm((3, 8, HALF), f32), vm((2, 2, 8, HALF), f32),
+        vm((8, 8, CH), f32), vm((8, 8, CH), f32), vm((8, 8, CH), f32),
+        vm((CHUNKS, CH, LANES), f32), vm((CHUNKS, CH, LANES), bf16), vm((CHUNKS, CH, LANES), bf16),
+        vm((CHUNKS, NX, 192, LANES), bf16), vm((CHUNKS, NX, 192, LANES), bf16),
+        vm((CHUNKS, 24, 8, LANES), f32), vm((CHUNKS, 24, 8, LANES), bf16), vm((CHUNKS, 8, 3, 8, LANES), bf16),
+        vm((CHUNKS, 3, 8, LANES), f32), vm((8, CHUNKS, 3, 8, LANES), f32),
+        vm((3, CHUNKS, 8, LANES), f32), vm((2, 2, CHUNKS, 8, LANES), f32),
         vm((CH,), f32), vm((CH,), f32),
-        pltpu.SemaphoreType.DMA((160,)), pltpu.SemaphoreType.DMA((160,)), pltpu.SemaphoreType.DMA((8,)),
+        pltpu.SemaphoreType.DMA((200,)), pltpu.SemaphoreType.DMA((200,)), pltpu.SemaphoreType.DMA((8,)),
     ]
     outs = [
         jax.ShapeDtypeStruct((ROWS, CH), bf16),

time: 75.5 us -> 70.5 us (0.934)
  the two profiles are of different devices: /device:TPU:1 before, /device:TPU:15 now
where the time goes in v3:
time: 70.5 us; the launch traced here: 70.4 us
  Pallas kernels  69.1 us (98%)
  between operations  1.29 us (2%)
    pallas_call x1, Pallas kernels, body(): pl.pallas_call(fused, out_shape=outs, in_specs=[anyspec, sspec, anyspec,...  68.2 us

profile of v3, /device:TPU:15, one launch (start us, length us, event | category | flops | bytes accessed | tf_op | source)
XLA Modules:
  0.0 70.4 jit_solution(13965994799498002258)
XLA Ops:
  1.3 68.2 %conformer_conv.1 = (bf16[128,768]{1,0:T(8,128)(2,1)S(1)}, bf16[128,1536]{1,0:T(8,128)(2,1)S(1)}, f32[12,768]{1,0:T(8,128)S(1)}, f32[31,768]{1,0:T(8,128)S(1)}, f32[768]{0:T(1024)S(1)}, /*index=5*/f32[768]{0:T(1024)S(1)}) custom-call(bf16[128,1536]{1,0:T(8,128)(2,1)} %bitcast.4, s32[1]{0:T(128)S(6)} %copy.13.len_ref, f32[31,768]{1,0:T(8,128)} %kern_hbm.1, ...), custom_call_target="tpu_custom_call" | custom-call | tf_op jit(solution)/shard_map/conformer_conv/pallas_call | solution.py:605
  69.5 0.9 %handed_on.1 = (bf16[128,768]{1,0:T(8,128)(2,1)}, bf16[128,1536]{1,0:T(8,128)(2,1)}, f32[12,768]{1,0:T(8,128)}, f32[31,768]{1,0:T(8,128)}, f32[768]{0:T(1024)}, /*index=5*/f32[768]{0:T(1024)}) custom-call(bf16[128,768]{1,0:T(8,128)(2,1)S(1)} %get-tuple-element.18.refs_0_, bf16[128,1536]{1,0:T(8,128)(2,1)S(1)} %get-tuple-element.19.refs_1_, ...), custom_call_target="tpu_custom_call" | custom-call | tf_op jit(solution)/shard_map/handed_on/pallas_call | solution.py:615

commit v4 on v3

--- a/solution.py
+++ b/solution.py
@@ -46,6 +46,7 @@
           glu, cot, kern, unit, conv, fac, dwide, da, act, out, gg, ub,
           wl, wr, wb, wfull, hs, hr, ds_, dr_, a1, a2, a3, b1, b2, b3, stat,
           kt, kr, k2, k3, kf, uq, ur, u2, gown, gsend, grc, gxs, gxr, gyf, gys, gyr, gz, gzr, fin, fb,
+          hz, hzr, hy, hyr, hx, hfin, hfb,
           gain_v, bias_v, ssem, rsem, lsem):
     dp = lax.axis_index("dp")
     ctx = lax.axis_index("ctx")
@@ -71,30 +72,39 @@
         return dev(z, y, j, core)
 
     sibling = dev(z, y, x, sib)
-    sends = [0]
-    recvs = [0]
+    used = [0, 0]
     pending = []
     cond = []
 
-    def rsems(n):
-        recvs[0] += n
-        return recvs[0] - n
+    def ssems(n=1):
+        used[0] += n
+        return used[0] - n
+
+    def rsems(n=1):
+        used[1] += n
+        return used[1] - n
+
+    def desc(src, dst, ssend, recv, target):
+        return pltpu.make_async_remote_copy(
+            src_ref=src, dst_ref=dst, send_sem=ssem.at[ssend], recv_sem=rsem.at[recv],
+            device_id=target, device_id_type=pl.DeviceIdType.MESH)
 
     def copy(src, dst, recv, target):
-        sends[0] += 1
-        return pltpu.make_async_remote_copy(
-            src_ref=src, dst_ref=dst, send_sem=ssem.at[sends[0] - 1], recv_sem=rsem.at[recv],
-            device_id=target, device_id_type=pl.DeviceIdType.MESH)
+        return desc(src, dst, ssems(), recv, target)
 
     def send(src, dst, recv, target):
         c = copy(src, dst, recv, target)
         c.start()
         pending.append(c)
 
+    def group(copies, total, recv):
+        sem = ssems()
+        for src, dst, target in copies:
+            desc(src, dst, sem, recv, target).start()
+        pending.append(desc(total, total, sem, recv, sibling))
+
     def arrived(dst, recv):
-        pltpu.make_async_remote_copy(
-            src_ref=dst, dst_ref=dst, send_sem=ssem.at[0], recv_sem=rsem.at[recv],
-            device_id=sibling, device_id_type=pl.DeviceIdType.MESH).wait_recv()
+        desc(dst, dst, 0, recv, sibling).wait_recv()
 
     def finish():
         for c in pending:
@@ -106,15 +116,19 @@
                     c.wait_send()
 
     def exchange(buf, me, where, n=8):
-        base = rsems(n)
+        recv = rsems()
+        others = buf.at[pl.ds(0, n - 1)]
+        group([(buf.at[me], buf.at[me], where(rem(me + d, n))) for d in range(1, n)], others, recv)
+        return lambda: arrived(others, recv)
+
+    def scatter(src_of, dst_of, total_src, total_dst, me, where, n=8):
+        recv = rsems()
+        copies = []
         for d in range(1, n):
-            send(buf.at[me], buf.at[me], base + d, where(rem(me + d, n)))
-
-        def done():
-            for d in range(1, n):
-                arrived(buf.at[rem(me + (n - d), n)], base + d)
-
-        return done
+            j = rem(me + d, n)
+            copies.append((src_of(j), dst_of(d), where(j)))
+        group(copies, total_src, recv)
+        return lambda: arrived(total_dst, recv)
 
     barrier = pltpu.get_barrier_semaphore()
     peers = [on_g(rem(g + d, 8)) for d in range(1, 8)]
@@ -148,8 +162,10 @@
 
     own_cols = pl.ds(pl.multiple_of(core * HALF, LANES), HALF)
     sib_cols = pl.ds(pl.multiple_of(sib * HALF, LANES), HALF)
-    w1, w2, w3, w4 = rsems(2), rsems(8), rsems(8), rsems(8)
+    w1, w2, w3, w4 = rsems(2), rsems(2), rsems(8), rsems(2)
     mine = wb.at[core, x, 0]
+    groups = ((0, 5), (5, 3))
+    w4_sems = []
     w1_sends = [copy(wl.at[:, sib_cols], wr.at[core], w1 + core, sibling)]
     for d in range(1, 4):
         y_ = rem(yh + d, 4) * 2 + yl
@@ -172,9 +188,10 @@
         arrived(wr.at[sib], w1 + sib)
         rows = jnp.concatenate([wr[0].astype(f32), wr[1].astype(f32)], 0)
         wb[core, x, 0] = rows.reshape(3, 8, HALF).astype(bf16)
-        for d in range(1, 8):
-            p = NEAR.index(8 - d)
-            send(mine, wb.at[core, x, p], w2 + p, on_z(rem(z + d, 8)))
+        for i, (first, size) in enumerate(groups):
+            places = range(max(first, 1), first + size)
+            group([(mine, wb.at[core, x, p], on_z(rem(z + 8 - NEAR[p], 8))) for p in places],
+                  wb.at[core, x, pl.ds(places[0], len(places))], w2 + i)
 
     loads[0].wait()
 
@@ -297,29 +314,34 @@
     a2[y] = packed(*merged(a1))
     a_done = exchange(a2, y, on_y)
 
-    groups = ((0, 5), (5, 3))
-
     def onward(i):
         first, size = groups[i]
-        for p in range(max(first, 1), first + size):
-            arrived(wb.at[core, x, p], w2 + p)
+        some = max(first, 1)
+        arrived(wb.at[core, x, pl.ds(some, first + size - some)], w2 + i)
         strip = wb.at[core, x, pl.ds(first, size)]
+        sem = ssems()
         for d in range(1, 4):
-            send(strip, strip, w3 + 4 * i + d, on_x(rem(x + d, 4)))
-        send(strip, strip, w4 + 4 * i, sibling)
+            desc(strip, strip, sem, w3 + 4 * i + d, on_x(rem(x + d, 4))).start()
+        pending.append(desc(wb.at[core, pl.ds(0, 3), pl.ds(first, size)],
+                            wb.at[core, pl.ds(0, 3), pl.ds(first, size)], sem, 0, sibling))
+        w4_sems.append(ssems())
+        desc(strip, strip, w4_sems[i], w4 + i, sibling).start()
 
     def across(i):
         first, size = groups[i]
         for d in range(1, 4):
             piece = wb.at[core, rem(x + (4 - d), 4), pl.ds(first, size)]
             arrived(piece, w3 + 4 * i + d)
-            send(piece, piece, w4 + 4 * i + d, sibling)
+            desc(piece, piece, w4_sems[i], w4 + i, sibling).start()
+        whole = wb.at[core, :, pl.ds(first, size)]
+        pending.append(desc(whole, whole, w4_sems[i], 0, sibling))
 
     onward(0)
     a_done()
     a3[z] = packed(*merged(a2))
     a_done = exchange(a3, z, on_z)
     onward(1)
+    uq_done = scatter(lambda j: uq.at[j], lambda d: ur.at[d], uq.at[pl.ds(0, 7)], ur.at[pl.ds(1, 7)], g, on_g)
     across(0)
     a_done()
     s, q, n = merged(a3)
@@ -341,13 +363,14 @@
         fac[c] = m * sp * (1.0 + pre * (1.0 - sp))
 
     across(1)
-    uq1 = rsems(8)
+    uq_done()
+    t = uq[g]
     for d in range(1, 8):
-        j = rem(g + d, 8)
-        send(uq.at[j], ur.at[d], uq1 + d, on_g(j))
+        t = t + ur[d]
+    u2[y] = t
+    u_done = exchange(u2, y, on_y)
     for i, (first, size) in enumerate(groups):
-        for d in range(4):
-            arrived(wb.at[sib, rem(x + (4 - d), 4), pl.ds(first, size)], w4 + 4 * i + d)
+        arrived(wb.at[sib, :, pl.ds(first, size)], w4 + i)
     for p in range(NZ):
         rows = pl.ds(pl.multiple_of(rem(z + NEAR[p], 8) * 96, 16), 96)
         for h in range(2):
@@ -369,7 +392,8 @@
 
     tn = (((0,), (0,)), ((), ()))
 
-    gc, gx, gy = rsems(CHUNKS), rsems(4 * CHUNKS), rsems(8 * CHUNKS)
+    gc, h3 = rsems(CHUNKS), rsems(CHUNKS)
+    h1_done, h2_done = {}, {}
 
     @tiles
     def _(c):
@@ -386,57 +410,75 @@
             kt[k // 4, pl.ds(k % 4, 1), at] = jnp.sum(d * unit[c, pl.ds(k + 1, ROWS), :], 0, keepdims=True)
         kt[7, 3:4, at] = jnp.zeros((1, LANES), f32)
 
-    for q in range(CHUNKS):
+    for q in (1, 2, 0):
         send(gsend.at[q], grc.at[q], gc + q, sibling)
-    k1 = rsems(8)
-    for d in range(1, 8):
-        j = rem(g + d, 8)
-        send(kt.at[j], kr.at[d], k1 + d, on_g(j))
+    k1_done = scatter(lambda j: kt.at[j], lambda d: kr.at[d], kt.at[pl.ds(0, 7)], kr.at[pl.ds(1, 7)], g, on_g)
     b_done()
-    b2[y] = summed(b1)
-    b_done = exchange(b2, y, on_y)
-    for d in range(1, 8):
-        arrived(ur.at[d], uq1 + d)
-    t = uq[g]
-    for d in range(1, 8):
-        t = t + ur[d]
-    u2[y] = t
-    u_done = exchange(u2, y, on_y)
-
-    for q in range(CHUNKS):
+    b2[z] = summed(b1)
+    b_done = exchange(b2, z, on_z)
+
+    for q in (1, 2, 0):
         arrived(grc.at[q], gc + q)
         t = gown[q] + grc[q].astype(f32)
         gown[q] = t
-        gxs[q] = t.astype(bf16).reshape(NX, 192, LANES)
+        if q == 0:
+            gxs[...] = t.astype(bf16).reshape(NX, 192, LANES)
+            gx_done = scatter(lambda j: gxs.at[j], lambda d: gxr.at[d],
+                              gxs.at[pl.ds(0, 3)], gxr.at[pl.ds(1, 3)], x, on_x, NX)
+        else:
+            hz[q] = t.astype(bf16).reshape(NZ, 96, LANES)
+            h1_done[q] = scatter(lambda j: hz.at[q, j], lambda d: hzr.at[q, d],
+                                 hz.at[q, pl.ds(0, 7)], hzr.at[q, pl.ds(1, 7)], z, on_z)
+
+    b_done()
+    b3[y] = summed(b2)
+    b_done = exchange(b3, y, on_y)
+
+    def x_part():
+        gx_done()
+        t = gown[0, pl.ds(pl.multiple_of(x * 192, 16), 192), :]
         for d in range(1, 4):
-            j = rem(x + d, 4)
-            send(gxs.at[q, j], gxr.at[q, d], gx + 4 * q + d, on_x(j))
-
-    b_done()
-    b3[z] = summed(b2)
-    b_done = exchange(b3, z, on_z)
-
-    def x_part(q):
-        for d in range(1, 4):
-            arrived(gxr.at[q, d], gx + 4 * q + d)
-        t = gown[q, pl.ds(pl.multiple_of(x * 192, 16), 192), :]
-        for d in range(1, 4):
-            t = t + gxr[q, d].astype(f32)
+            t = t + gxr[d].astype(f32)
         t = t.reshape(24, 8, LANES)
-        gyf[q] = t
-        gys[q] = t.astype(bf16)
+        gyf[...] = t
+        gys[...] = t.astype(bf16)
+        return scatter(lambda j: gys.at[pl.ds(rem(j, 2) * 12 + div(j, 2) * 3, 3)], lambda d: gyr.at[d],
+                       gyr.at[pl.ds(0, 7)], gyr.at[pl.ds(1, 7)], y, on_y)
+
+    def z_part(q):
+        h1_done[q]()
+        t = gown[q, pl.ds(pl.multiple_of(z * 96, 16), 96), :]
         for d in range(1, 8):
-            j = rem(y + d, 8)
-            send(gys.at[q, pl.ds(rem(j, 2) * 12 + div(j, 2) * 3, 3)], gyr.at[q, d], gy + 8 * q + d, on_y(j))
-
-    for d in range(1, 8):
-        arrived(kr.at[d], k1 + d)
+            t = t + hzr[q, d].astype(f32)
+        hy[q] = t.reshape(12, 8, LANES).astype(bf16)
+        h2_done[q] = scatter(lambda j: hy.at[q, pl.ds(div(j, 2) * 3, 3)], lambda d: hyr.at[q, y],
+                             hyr.at[q, pl.ds(0, 7)], hyr.at[q, pl.ds(0, 7)], y, on_y)
+        hyr[q, y] = hy[q, pl.ds(yh * 3, 3)]
+
+    def zy_part(q):
+        h2_done[q]()
+        t = hyr[q, 0].astype(f32)
+        for i in range(1, 8):
+            t = t + hyr[q, i].astype(f32)
+        hx[q, x] = t
+        return exchange(hx.at[q], x, on_x, NX)
+
+    def zyx_part(q, done):
+        done()
+        t = hx[q, 0]
+        for i in range(1, NX):
+            t = t + hx[q, i]
+        hfin[q] = t * stat[3:4, 0:LANES].reshape(1, 1, LANES)
+        send(hfin.at[q, pl.ds(sib, 2)], hfb.at[core, q], h3 + q, sibling)
+        hfb[core, q] = hfin[q, pl.ds(core, 2)]
+
+    k1_done()
     t = kt[g]
     for d in range(1, 8):
         t = t + kr[d]
     k2[y] = t
     k_done = exchange(k2, y, on_y)
-    x_part(0)
+    gy_done = x_part()
     for h in range(2):
         out[:, h * HALF:(h + 1) * HALF] = jnp.dot(act[...], wfull[h], preferred_element_type=f32).astype(bf16)
     store_out = pltpu.make_async_copy(out, out_hbm, lsem.at[6])
@@ -467,20 +509,27 @@
     k3[z] = (stat[6:7] * inv) * (
         summed(k2) - stat[4:5] * u_rows - stat[5:6] * (inv * (q_rows - stat[0:1] * u_rows)))
     k_done = exchange(k3, z, on_z)
-    x_part(1)
-    x_part(2)
+    z_part(1)
+    z_part(2)
 
     owner = 2 * x + yl
-    gzb = rsems(8)
+    gzb = rsems()
     slot = rem(z + 8 - owner, 8)
 
-    def y_part(q):
+    def y_part():
+        gy_done()
+        t = gyf[pl.ds(yl * 12 + yh * 3, 3)]
         for d in range(1, 8):
-            arrived(gyr.at[q, d], gy + 8 * q + d)
-        t = gyf[q, pl.ds(yl * 12 + yh * 3, 3)]
-        for d in range(1, 8):
-            t = t + gyr[q, d].astype(f32)
-        gz[q] = t
+            t = t + gyr[d].astype(f32)
+        gz[...] = t
+
+    y_part()
+    to_owner = copy(gz, gzr.at[slot], gzb, on_z(owner))
+    cond.append((z != owner, [to_owner]))
+
+    @pl.when(z != owner)
+    def _():
+        to_owner.start()
 
     halo_done()
 
@@ -501,18 +550,12 @@
     store_gg = pltpu.make_async_copy(gg, gg_hbm, lsem.at[7])
     store_gg.start()
 
-    for q in range(CHUNKS):
-        y_part(q)
-    to_owner = copy(gz, gzr.at[slot], gzb + slot, on_z(owner))
-    cond.append((z != owner, [to_owner]))
-
-    @pl.when(z != owner)
-    def _():
-        to_owner.start()
-
+    x1_done = zy_part(1)
     k_done()
     kf[g] = summed(k3) * stat[3:4]
     k_done = exchange(kf, g, on_g)
+    x2_done = zy_part(2)
+    zyx_part(1, x1_done)
 
     fbb = rsems(2)
     spread = []
@@ -524,19 +567,16 @@
 
     @pl.when(z == owner)
     def _():
+        arrived(gzr.at[pl.ds(1, 7)], gzb)
+        t = gz[...]
         for d in range(1, 8):
-            arrived(gzr.at[d], gzb + d)
-        for q in range(CHUNKS):
-            t = gz[q]
-            for d in range(1, 8):
-                t = t + gzr[d, q]
-            t = t * stat[3:4, 0:LANES].reshape(1, 1, LANES)
-            for u in range(3):
-                fin[u, q] = t[u]
+            t = t + gzr[d]
+        fin[...] = t * stat[3:4, 0:LANES].reshape(1, 1, LANES)
         for c in spread:
             c.start()
         fb[core] = fin[pl.ds(core, 2)]
 
+    zyx_part(2, x2_done)
     k_done()
     for j in range(8):
         w = 4 if j < 7 else 3
@@ -547,9 +587,12 @@
         arrived(fb.at[core], fbb + core)
 
     arrived(fb.at[sib], fbb + sib)
+    for q in (1, 2):
+        arrived(hfb.at[sib, q], h3 + q)
     for h in range(2):
         for q in range(CHUNKS):
-            v = jnp.concatenate([fb[h, 0, q], fb[h, 1, q]], 0)
+            v = fb[h] if q == 0 else hfb[h, q]
+            v = v.reshape(16, LANES)
             gp_ref[:, pl.ds(h * HALF + q * LANES, LANES)] = jnp.where(core == 0, v[0:BLOCK], v[16 - BLOCK:16])
 
     finish()
@@ -587,12 +630,15 @@
         vm((8, 4, CH), f32), vm((8, 4, CH), f32), vm((8, 4, CH), f32), vm((8, 4, CH), f32), vm((8, 4, CH), f32),
         vm((8, 8, CH), f32), vm((8, 8, CH), f32), vm((8, 8, CH), f32),
         vm((CHUNKS, CH, LANES), f32), vm((CHUNKS, CH, LANES), bf16), vm((CHUNKS, CH, LANES), bf16),
-        vm((CHUNKS, NX, 192, LANES), bf16), vm((CHUNKS, NX, 192, LANES), bf16),
-        vm((CHUNKS, 24, 8, LANES), f32), vm((CHUNKS, 24, 8, LANES), bf16), vm((CHUNKS, 8, 3, 8, LANES), bf16),
-        vm((CHUNKS, 3, 8, LANES), f32), vm((8, CHUNKS, 3, 8, LANES), f32),
-        vm((3, CHUNKS, 8, LANES), f32), vm((2, 2, CHUNKS, 8, LANES), f32),
+        vm((NX, 192, LANES), bf16), vm((NX, 192, LANES), bf16),
+        vm((24, 8, LANES), f32), vm((24, 8, LANES), bf16), vm((8, 3, 8, LANES), bf16),
+        vm((3, 8, LANES), f32), vm((8, 3, 8, LANES), f32),
+        vm((3, 8, LANES), f32), vm((2, 2, 8, LANES), f32),
+        vm((CHUNKS, NZ, 96, LANES), bf16), vm((CHUNKS, NZ, 96, LANES), bf16),
+        vm((CHUNKS, 12, 8, LANES), bf16), vm((CHUNKS, 8, 3, 8, LANES), bf16),
+        vm((CHUNKS, NX, 3, 8, LANES), f32), vm((CHUNKS, 3, 8, LANES), f32), vm((2, CHUNKS, 2, 8, LANES), f32),
         vm((CH,), f32), vm((CH,), f32),
-        pltpu.SemaphoreType.DMA((200,)), pltpu.SemaphoreType.DMA((200,)), pltpu.SemaphoreType.DMA((8,)),
+        pltpu.SemaphoreType.DMA((64,)), pltpu.SemaphoreType.DMA((64,)), pltpu.SemaphoreType.DMA((8,)),
     ]
     outs = [
         jax.ShapeDtypeStruct((ROWS, CH), bf16),

time: 70.5 us -> 65.9 us (0.935)
  the two profiles are of different devices: /device:TPU:15 before, /device:TPU:1 now
where the time goes in v4:
time: 65.9 us; the launch traced here: 65.7 us
  Pallas kernels  64.5 us (98%)
  between operations  1.29 us (2%)
    pallas_call x1, Pallas kernels, body(): pl.pallas_call(fused, out_shape=outs, in_specs=[anyspec, sspec, anyspec,...  63.5 us

profile of v4, /device:TPU:1, one launch (start us, length us, event | category | flops | bytes accessed | tf_op | source)
XLA Modules:
  0.0 65.7 jit_solution(3706923921651997863)
XLA Ops:
  1.3 63.5 %conformer_conv.1 = (bf16[128,768]{1,0:T(8,128)(2,1)S(1)}, bf16[128,1536]{1,0:T(8,128)(2,1)S(1)}, f32[12,768]{1,0:T(8,128)S(1)}, f32[31,768]{1,0:T(8,128)S(1)}, f32[768]{0:T(1024)S(1)}, /*index=5*/f32[768]{0:T(1024)S(1)}) custom-call(bf16[128,1536]{1,0:T(8,128)(2,1)} %bitcast.4, s32[1]{0:T(128)S(6)} %copy.13.len_ref, f32[31,768]{1,0:T(8,128)} %kern_hbm.1, ...), custom_call_target="tpu_custom_call" | custom-call | tf_op jit(solution)/shard_map/conformer_conv/pallas_call | solution.py:651
  64.8 0.9 %handed_on.1 = (bf16[128,768]{1,0:T(8,128)(2,1)}, bf16[128,1536]{1,0:T(8,128)(2,1)}, f32[12,768]{1,0:T(8,128)}, f32[31,768]{1,0:T(8,128)}, f32[768]{0:T(1024)}, /*index=5*/f32[768]{0:T(1024)}) custom-call(bf16[128,768]{1,0:T(8,128)(2,1)S(1)} %get-tuple-element.18.refs_0_, bf16[128,1536]{1,0:T(8,128)(2,1)S(1)} %get-tuple-element.19.refs_1_, ...), custom_call_target="tpu_custom_call" | custom-call | tf_op jit(solution)/shard_map/handed_on/pallas_call | solution.py:661

commit v5 on v4

--- a/solution.py
+++ b/solution.py
@@ -45,7 +45,7 @@
           out_hbm, gg_hbm, gp_ref, gk_ref, gn_ref, gb_ref,
           glu, cot, kern, unit, conv, fac, dwide, da, act, out, gg, ub,
           wl, wr, wb, wfull, hs, hr, ds_, dr_, a1, a2, a3, b1, b2, b3, stat,
-          kt, kr, k2, k3, kf, uq, ur, u2, gown, gsend, grc, gxs, gxr, gyf, gys, gyr, gz, gzr, fin, fb,
+          kt, kr, k2, k3, kf, uq, ur, u2, gown, gsend, grc, gxs, gxr, gyf, gys, gyr, gz, gzs, gzr, fin, fb,
           hz, hzr, hy, hyr, hx, hfin, hfb,
           gain_v, bias_v, ssem, rsem, lsem):
     dp = lax.axis_index("dp")
@@ -337,10 +337,10 @@
         pending.append(desc(whole, whole, w4_sems[i], 0, sibling))
 
     onward(0)
+    onward(1)
     a_done()
     a3[z] = packed(*merged(a2))
     a_done = exchange(a3, z, on_z)
-    onward(1)
     uq_done = scatter(lambda j: uq.at[j], lambda d: ur.at[d], uq.at[pl.ds(0, 7)], ur.at[pl.ds(1, 7)], g, on_g)
     across(0)
     a_done()
@@ -363,18 +363,18 @@
         fac[c] = m * sp * (1.0 + pre * (1.0 - sp))
 
     across(1)
+    for i, (first, size) in enumerate(groups):
+        arrived(wb.at[sib, :, pl.ds(first, size)], w4 + i)
+    for p in range(NZ):
+        rows = pl.ds(pl.multiple_of(rem(z + NEAR[p], 8) * 96, 16), 96)
+        for h in range(2):
+            wfull[h, rows, :] = wb[h, :, p].astype(f32).reshape(96, HALF).astype(bf16)
     uq_done()
     t = uq[g]
     for d in range(1, 8):
         t = t + ur[d]
     u2[y] = t
     u_done = exchange(u2, y, on_y)
-    for i, (first, size) in enumerate(groups):
-        arrived(wb.at[sib, :, pl.ds(first, size)], w4 + i)
-    for p in range(NZ):
-        rows = pl.ds(pl.multiple_of(rem(z + NEAR[p], 8) * 96, 16), 96)
-        for h in range(2):
-            wfull[h, rows, :] = wb[h, :, p].astype(f32).reshape(96, HALF).astype(bf16)
     loads[2].wait()
     nt = (((1,), (1,)), ((), ()))
     da[...] = (lax.dot_general(cot[:, 0:HALF], wfull[0], nt, preferred_element_type=f32)
@@ -410,40 +410,53 @@
             kt[k // 4, pl.ds(k % 4, 1), at] = jnp.sum(d * unit[c, pl.ds(k + 1, ROWS), :], 0, keepdims=True)
         kt[7, 3:4, at] = jnp.zeros((1, LANES), f32)
 
-    for q in (1, 2, 0):
+    for q in range(CHUNKS):
         send(gsend.at[q], grc.at[q], gc + q, sibling)
     k1_done = scatter(lambda j: kt.at[j], lambda d: kr.at[d], kt.at[pl.ds(0, 7)], kr.at[pl.ds(1, 7)], g, on_g)
+    gx_done = []
+
+    def x_send(q):
+        return scatter(lambda j: gxs.at[q, j], lambda d: gxr.at[q, d],
+                       gxs.at[q, pl.ds(0, 3)], gxr.at[q, pl.ds(1, 3)], x, on_x, NX)
+
+    for q in (0, 1):
+        arrived(grc.at[q], gc + q)
+        t = gown[q] + grc[q].astype(f32)
+        gown[q] = t
+        gxs[q] = t.astype(bf16).reshape(NX, 192, LANES)
+        gx_done.append(x_send(q))
+
     b_done()
     b2[z] = summed(b1)
     b_done = exchange(b2, z, on_z)
 
-    for q in (1, 2, 0):
-        arrived(grc.at[q], gc + q)
-        t = gown[q] + grc[q].astype(f32)
-        gown[q] = t
-        if q == 0:
-            gxs[...] = t.astype(bf16).reshape(NX, 192, LANES)
-            gx_done = scatter(lambda j: gxs.at[j], lambda d: gxr.at[d],
-                              gxs.at[pl.ds(0, 3)], gxr.at[pl.ds(1, 3)], x, on_x, NX)
-        else:
-            hz[q] = t.astype(bf16).reshape(NZ, 96, LANES)
-            h1_done[q] = scatter(lambda j: hz.at[q, j], lambda d: hzr.at[q, d],
-                                 hz.at[q, pl.ds(0, 7)], hzr.at[q, pl.ds(1, 7)], z, on_z)
-
+    arrived(grc.at[2], gc + 2)
+    t = gown[2] + grc[2].astype(f32)
+    gown[2] = t
+    hz[2] = t.astype(bf16).reshape(NZ, 96, LANES)
+    h1_done[2] = scatter(lambda j: hz.at[2, j], lambda d: hzr.at[2, d],
+                         hz.at[2, pl.ds(0, 7)], hzr.at[2, pl.ds(1, 7)], z, on_z)
+
+    k1_done()
+    t = kt[g]
+    for d in range(1, 8):
+        t = t + kr[d]
+    k2[y] = t
+    k_done = exchange(k2, y, on_y)
     b_done()
     b3[y] = summed(b2)
     b_done = exchange(b3, y, on_y)
 
-    def x_part():
-        gx_done()
-        t = gown[0, pl.ds(pl.multiple_of(x * 192, 16), 192), :]
+    def x_part(q):
+        gx_done[q]()
+        t = gown[q, pl.ds(pl.multiple_of(x * 192, 16), 192), :]
         for d in range(1, 4):
-            t = t + gxr[d].astype(f32)
+            t = t + gxr[q, d].astype(f32)
         t = t.reshape(24, 8, LANES)
-        gyf[...] = t
-        gys[...] = t.astype(bf16)
-        return scatter(lambda j: gys.at[pl.ds(rem(j, 2) * 12 + div(j, 2) * 3, 3)], lambda d: gyr.at[d],
-                       gyr.at[pl.ds(0, 7)], gyr.at[pl.ds(1, 7)], y, on_y)
+        gyf[q] = t
+        gys[q] = t.astype(bf16)
+        return scatter(lambda j: gys.at[q, pl.ds(rem(j, 2) * 12 + div(j, 2) * 3, 3)], lambda d: gyr.at[q, d],
+                       gyr.at[q, pl.ds(0, 7)], gyr.at[q, pl.ds(1, 7)], y, on_y)
 
     def z_part(q):
         h1_done[q]()
@@ -472,13 +485,7 @@
         send(hfin.at[q, pl.ds(sib, 2)], hfb.at[core, q], h3 + q, sibling)
         hfb[core, q] = hfin[q, pl.ds(core, 2)]
 
-    k1_done()
-    t = kt[g]
-    for d in range(1, 8):
-        t = t + kr[d]
-    k2[y] = t
-    k_done = exchange(k2, y, on_y)
-    gy_done = x_part()
+    gy_done = [x_part(0), x_part(1)]
     for h in range(2):
         out[:, h * HALF:(h + 1) * HALF] = jnp.dot(act[...], wfull[h], preferred_element_type=f32).astype(bf16)
     store_out = pltpu.make_async_copy(out, out_hbm, lsem.at[6])
@@ -509,22 +516,23 @@
     k3[z] = (stat[6:7] * inv) * (
         summed(k2) - stat[4:5] * u_rows - stat[5:6] * (inv * (q_rows - stat[0:1] * u_rows)))
     k_done = exchange(k3, z, on_z)
-    z_part(1)
-    z_part(2)
 
     owner = 2 * x + yl
     gzb = rsems()
     slot = rem(z + 8 - owner, 8)
 
-    def y_part():
-        gy_done()
-        t = gyf[pl.ds(yl * 12 + yh * 3, 3)]
+    def y_part(q):
+        gy_done[q]()
+        t = gyf[q, pl.ds(yl * 12 + yh * 3, 3)]
         for d in range(1, 8):
-            t = t + gyr[d].astype(f32)
-        gz[...] = t
-
-    y_part()
-    to_owner = copy(gz, gzr.at[slot], gzb, on_z(owner))
+            t = t + gyr[q, d].astype(f32)
+        gz[q] = t
+        gzs[q] = t.astype(bf16)
+
+    z_part(2)
+    y_part(0)
+    y_part(1)
+    to_owner = copy(gzs, gzr.at[slot], gzb, on_z(owner))
     cond.append((z != owner, [to_owner]))
 
     @pl.when(z != owner)
@@ -550,12 +558,10 @@
     store_gg = pltpu.make_async_copy(gg, gg_hbm, lsem.at[7])
     store_gg.start()
 
-    x1_done = zy_part(1)
+    x2_done = zy_part(2)
     k_done()
     kf[g] = summed(k3) * stat[3:4]
     k_done = exchange(kf, g, on_g)
-    x2_done = zy_part(2)
-    zyx_part(1, x1_done)
 
     fbb = rsems(2)
     spread = []
@@ -568,10 +574,13 @@
     @pl.when(z == owner)
     def _():
         arrived(gzr.at[pl.ds(1, 7)], gzb)
-        t = gz[...]
-        for d in range(1, 8):
-            t = t + gzr[d]
-        fin[...] = t * stat[3:4, 0:LANES].reshape(1, 1, LANES)
+        for q in (0, 1):
+            t = gz[q]
+            for d in range(1, 8):
+                t = t + gzr[d, q].astype(f32)
+            t = t * stat[3:4, 0:LANES].reshape(1, 1, LANES)
+            for u in range(3):
+                fin[u, q] = t[u]
         for c in spread:
             c.start()
         fb[core] = fin[pl.ds(core, 2)]
@@ -587,12 +596,10 @@
         arrived(fb.at[core], fbb + core)
 
     arrived(fb.at[sib], fbb + sib)
-    for q in (1, 2):
-        arrived(hfb.at[sib, q], h3 + q)
+    arrived(hfb.at[sib, 2], h3 + 2)
     for h in range(2):
         for q in range(CHUNKS):
-            v = fb[h] if q == 0 else hfb[h, q]
-            v = v.reshape(16, LANES)
+            v = jnp.concatenate([fb[h, 0, q], fb[h, 1, q]], 0) if q < 2 else hfb[h, q].reshape(16, LANES)
             gp_ref[:, pl.ds(h * HALF + q * LANES, LANES)] = jnp.where(core == 0, v[0:BLOCK], v[16 - BLOCK:16])
 
     finish()
@@ -630,10 +637,10 @@
         vm((8, 4, CH), f32), vm((8, 4, CH), f32), vm((8, 4, CH), f32), vm((8, 4, CH), f32), vm((8, 4, CH), f32),
         vm((8, 8, CH), f32), vm((8, 8, CH), f32), vm((8, 8, CH), f32),
         vm((CHUNKS, CH, LANES), f32), vm((CHUNKS, CH, LANES), bf16), vm((CHUNKS, CH, LANES), bf16),
-        vm((NX, 192, LANES), bf16), vm((NX, 192, LANES), bf16),
-        vm((24, 8, LANES), f32), vm((24, 8, LANES), bf16), vm((8, 3, 8, LANES), bf16),
-        vm((3, 8, LANES), f32), vm((8, 3, 8, LANES), f32),
-        vm((3, 8, LANES), f32), vm((2, 2, 8, LANES), f32),
+        vm((2, NX, 192, LANES), bf16), vm((2, NX, 192, LANES), bf16),
+        vm((2, 24, 8, LANES), f32), vm((2, 24, 8, LANES), bf16), vm((2, 8, 3, 8, LANES), bf16),
+        vm((2, 3, 8, LANES), f32), vm((2, 3, 8, LANES), bf16), vm((8, 2, 3, 8, LANES), bf16),
+        vm((3, 2, 8, LANES), f32), vm((2, 2, 2, 8, LANES), f32),
         vm((CHUNKS, NZ, 96, LANES), bf16), vm((CHUNKS, NZ, 96, LANES), bf16),
         vm((CHUNKS, 12, 8, LANES), bf16), vm((CHUNKS, 8, 3, 8, LANES), bf16),
         vm((CHUNKS, NX, 3, 8, LANES), f32), vm((CHUNKS, 3, 8, LANES), f32), vm((2, CHUNKS, 2, 8, LANES), f32),

time: 65.9 us -> 64.5 us (0.979)
  Pallas kernels: 64.5 us -> 63 us
    pallas_call x1, Pallas kernels: 63.5 us -> 62.1 us  [body(): pl.pallas_call(fused, out_shape=outs, in_specs=[anyspec, sspec, anyspec,...]
where the time goes in v5:
time: 64.5 us; the launch traced here: 64.3 us
  Pallas kernels  63 us (98%)
  between operations  1.29 us (2%)
    pallas_call x1, Pallas kernels, body(): pl.pallas_call(fused, out_shape=outs, in_specs=[anyspec, sspec, anyspec,...  62.1 us

profile of v5, /device:TPU:1, one launch (start us, length us, event | category | flops | bytes accessed | tf_op | source)
XLA Modules:
  0.0 64.3 jit_solution(14608663263027821953)
XLA Ops:
  1.3 62.1 %conformer_conv.1 = (bf16[128,768]{1,0:T(8,128)(2,1)S(1)}, bf16[128,1536]{1,0:T(8,128)(2,1)S(1)}, f32[12,768]{1,0:T(8,128)S(1)}, f32[31,768]{1,0:T(8,128)S(1)}, f32[768]{0:T(1024)S(1)}, /*index=5*/f32[768]{0:T(1024)S(1)}) custom-call(bf16[128,1536]{1,0:T(8,128)(2,1)} %bitcast.4, s32[1]{0:T(128)S(6)} %copy.13.len_ref, f32[31,768]{1,0:T(8,128)} %kern_hbm.1, ...), custom_call_target="tpu_custom_call" | custom-call | tf_op jit(solution)/shard_map/conformer_conv/pallas_call | solution.py:658
  63.4 0.9 %handed_on.1 = (bf16[128,768]{1,0:T(8,128)(2,1)}, bf16[128,1536]{1,0:T(8,128)(2,1)}, f32[12,768]{1,0:T(8,128)}, f32[31,768]{1,0:T(8,128)}, f32[768]{0:T(1024)}, /*index=5*/f32[768]{0:T(1024)}) custom-call(bf16[128,768]{1,0:T(8,128)(2,1)S(1)} %get-tuple-element.18.refs_0_, bf16[128,1536]{1,0:T(8,128)(2,1)S(1)} %get-tuple-element.19.refs_1_, ...), custom_call_target="tpu_custom_call" | custom-call | tf_op jit(solution)/shard_map/handed_on/pallas_call | solution.py:668

commit v6 on v5

--- a/solution.py
+++ b/solution.py
@@ -490,6 +490,7 @@
         out[:, h * HALF:(h + 1) * HALF] = jnp.dot(act[...], wfull[h], preferred_element_type=f32).astype(bf16)
     store_out = pltpu.make_async_copy(out, out_hbm, lsem.at[6])
     store_out.start()
+    z_part(2)
     b_done()
     sums = summed(b3)
     gb_ref[...] = (sums[0:1] * stat[3:4]).reshape(CH)
@@ -529,7 +530,6 @@
         gz[q] = t
         gzs[q] = t.astype(bf16)
 
-    z_part(2)
     y_part(0)
     y_part(1)
     to_owner = copy(gzs, gzr.at[slot], gzb, on_z(owner))
@@ -540,6 +540,7 @@
         to_owner.start()
 
     halo_done()
+    x2_done = zy_part(2)
 
     @tiles
     def _(c):
@@ -558,10 +559,11 @@
     store_gg = pltpu.make_async_copy(gg, gg_hbm, lsem.at[7])
     store_gg.start()
 
-    x2_done = zy_part(2)
     k_done()
     kf[g] = summed(k3) * stat[3:4]
     k_done = exchange(kf, g, on_g)
+
+    zyx_part(2, x2_done)
 
     fbb = rsems(2)
     spread = []
@@ -585,7 +587,6 @@
             c.start()
         fb[core] = fin[pl.ds(core, 2)]
 
-    zyx_part(2, x2_done)
     k_done()
     for j in range(8):
         w = 4 if j < 7 else 3
@@ -645,7 +646,7 @@
         vm((CHUNKS, 12, 8, LANES), bf16), vm((CHUNKS, 8, 3, 8, LANES), bf16),
         vm((CHUNKS, NX, 3, 8, LANES), f32), vm((CHUNKS, 3, 8, LANES), f32), vm((2, CHUNKS, 2, 8, LANES), f32),
         vm((CH,), f32), vm((CH,), f32),
-        pltpu.SemaphoreType.DMA((64,)), pltpu.SemaphoreType.DMA((64,)), pltpu.SemaphoreType.DMA((8,)),
+        pltpu.SemaphoreType.DMA((56,)), pltpu.SemaphoreType.DMA((46,)), pltpu.SemaphoreType.DMA((8,)),
     ]
     outs = [
         jax.ShapeDtypeStruct((ROWS, CH), bf16),

time: 64.5 us -> 63.4 us (0.983)
  Pallas kernels: 63 us -> 61.9 us
    pallas_call x1, Pallas kernels: 62.1 us -> 61 us  [body(): pl.pallas_call(fused, out_shape=outs, in_specs=[anyspec, sspec, anyspec,...]
where the time goes in v6:
time: 63.4 us; the launch traced here: 63.2 us
  Pallas kernels  61.9 us (98%)
  between operations  1.29 us (2%)
    pallas_call x1, Pallas kernels, body(): pl.pallas_call(fused, out_shape=outs, in_specs=[anyspec, sspec, anyspec,...  61 us

profile of v6, /device:TPU:1, one launch (start us, length us, event | category | flops | bytes accessed | tf_op | source)
XLA Modules:
  0.0 63.2 jit_solution(9899306819515743152)
XLA Ops:
  1.3 61.0 %conformer_conv.1 = (bf16[128,768]{1,0:T(8,128)(2,1)S(1)}, bf16[128,1536]{1,0:T(8,128)(2,1)S(1)}, f32[12,768]{1,0:T(8,128)S(1)}, f32[31,768]{1,0:T(8,128)S(1)}, f32[768]{0:T(1024)S(1)}, /*index=5*/f32[768]{0:T(1024)S(1)}) custom-call(bf16[128,1536]{1,0:T(8,128)(2,1)} %bitcast.4, s32[1]{0:T(128)S(6)} %copy.13.len_ref, f32[31,768]{1,0:T(8,128)} %kern_hbm.1, ...), custom_call_target="tpu_custom_call" | custom-call | tf_op jit(solution)/shard_map/conformer_conv/pallas_call | solution.py:659
  62.3 0.9 %handed_on.1 = (bf16[128,768]{1,0:T(8,128)(2,1)}, bf16[128,1536]{1,0:T(8,128)(2,1)}, f32[12,768]{1,0:T(8,128)}, f32[31,768]{1,0:T(8,128)}, f32[768]{0:T(1024)}, /*index=5*/f32[768]{0:T(1024)}) custom-call(bf16[128,768]{1,0:T(8,128)(2,1)S(1)} %get-tuple-element.18.refs_0_, bf16[128,1536]{1,0:T(8,128)(2,1)S(1)} %get-tuple-element.19.refs_1_, ...), custom_call_target="tpu_custom_call" | custom-call | tf_op jit(solution)/shard_map/handed_on/pallas_call | solution.py:669

commit v7 on v6

--- a/solution.py
+++ b/solution.py
@@ -31,6 +31,10 @@
 
 def lanes_of(c, first=0):
     return pl.ds(pl.multiple_of(first + c * LANES, LANES), LANES)
+
+
+def farthest(n):
+    return sorted(range(1, n), key=lambda d: -min(d, n - d))
 
 
 def tiles(fn):
@@ -118,13 +122,13 @@
     def exchange(buf, me, where, n=8):
         recv = rsems()
         others = buf.at[pl.ds(0, n - 1)]
-        group([(buf.at[me], buf.at[me], where(rem(me + d, n))) for d in range(1, n)], others, recv)
+        group([(buf.at[me], buf.at[me], where(rem(me + d, n))) for d in farthest(n)], others, recv)
         return lambda: arrived(others, recv)
 
     def scatter(src_of, dst_of, total_src, total_dst, me, where, n=8):
         recv = rsems()
         copies = []
-        for d in range(1, n):
+        for d in farthest(n):
             j = rem(me + d, n)
             copies.append((src_of(j), dst_of(d), where(j)))
         group(copies, total_src, recv)

time: 63.4 us -> 62.4 us (0.984)
  Pallas kernels: 61.9 us -> 60.6 us
    pallas_call x1, Pallas kernels: 61 us -> 59.7 us  [body(): pl.pallas_call(fused, out_shape=outs, in_specs=[anyspec, sspec, anyspec,...]
where the time goes in v7:
time: 62.4 us; the launch traced here: 61.9 us
  Pallas kernels  60.6 us (97%)
  between operations  1.29 us (2%)
    pallas_call x1, Pallas kernels, body(): pl.pallas_call(fused, out_shape=outs, in_specs=[anyspec, sspec, anyspec,...  59.7 us

profile of v7, /device:TPU:1, one launch (start us, length us, event | category | flops | bytes accessed | tf_op | source)
XLA Modules:
  0.0 61.9 jit_solution(7911342782328693307)
XLA Ops:
  1.3 59.7 %conformer_conv.1 = (bf16[128,768]{1,0:T(8,128)(2,1)S(1)}, bf16[128,1536]{1,0:T(8,128)(2,1)S(1)}, f32[12,768]{1,0:T(8,128)S(1)}, f32[31,768]{1,0:T(8,128)S(1)}, f32[768]{0:T(1024)S(1)}, /*index=5*/f32[768]{0:T(1024)S(1)}) custom-call(bf16[128,1536]{1,0:T(8,128)(2,1)} %bitcast.4, s32[1]{0:T(128)S(6)} %copy.13.len_ref, f32[31,768]{1,0:T(8,128)} %kern_hbm.1, ...), custom_call_target="tpu_custom_call" | custom-call | tf_op jit(solution)/shard_map/conformer_conv/pallas_call | solution.py:663
  60.9 0.9 %handed_on.1 = (bf16[128,768]{1,0:T(8,128)(2,1)}, bf16[128,1536]{1,0:T(8,128)(2,1)}, f32[12,768]{1,0:T(8,128)}, f32[31,768]{1,0:T(8,128)}, f32[768]{0:T(1024)}, /*index=5*/f32[768]{0:T(1024)}) custom-call(bf16[128,768]{1,0:T(8,128)(2,1)S(1)} %get-tuple-element.18.refs_0_, bf16[128,1536]{1,0:T(8,128)(2,1)S(1)} %get-tuple-element.19.refs_1_, ...), custom_call_target="tpu_custom_call" | custom-call | tf_op jit(solution)/shard_map/handed_on/pallas_call | solution.py:673
